TPU v7x, 128 devices: a whole 4x4x4 slice. The times are simulated.
128 devices in a mesh: dp: 4 (over x_lo, core), ctx: 32 (over x_hi, z, y).
Axes of the slice: x: 4 (x_hi: 2, x_lo: 2; x = x_hi * 2 + x_lo), y: 4, z: 4, core: 2. Of those that a mesh axis runs over, the one named last changes fastest.
Arguments:
- projections: bfloat16 [2, 16384, 4352], P(None, ('dp', 'ctx')), may hold values from -6 to 6
- dt_raw: bfloat16 [2, 16384, 32], P(None, ('dp', 'ctx')), may hold values from -6 to 6
- a_log: float32 [32], replicated, as said below
- dt_bias: float32 [32], replicated, may hold values from -1 to 0.5
- skip_gain: float32 [32], replicated, may hold values from 0.5 to 1.5
- norm_gain: float32 [2048], replicated, may hold values from 0.25 to 1.75
- w_out: bfloat16 [2048, 2048], replicated, may hold values from -0.125 to 0.125
- base_ids: int32 [16384], P(('dp', 'ctx')), may hold values from 0 to 4
- cotangent: bfloat16 [16384, 2048], P(('dp', 'ctx')), may hold values from -24 to 24
Outputs:
- mixed_out: bfloat16 [16384, 2048], P(('dp', 'ctx'))
- d_proj: bfloat16 [2, 16384, 4352], P(None, ('dp', 'ctx'))
- d_dt_raw: bfloat16 [2, 16384, 32], P(None, ('dp', 'ctx'))
- d_w_out: float32 [2048, 2048], P(('dp', 'ctx'))
- d_heads: float32 [3, 32], replicated
- d_gain: float32 [2048], replicated
Inputs may be any that keep to these rules, and one draw needn't show every extreme that they name: `a_log`: each entry is the natural logarithm of a positive per-head rate.
All inputs are finite; a program needn't handle non-finite values.
Results may differ from a plain program's by a relative error of at most 0.0059.
Values may be sent and summed in bfloat16 or wider, within the bound.
A program may use at most 320 MiB of HBM per device.

v0:
```python
import functools

import jax
import jax.numpy as jnp
from jax import lax
from jax.experimental import pallas as pl
from jax.experimental.pallas import tpu as pltpu
from jax.sharding import PartitionSpec as P

MESH = pl.DeviceIdType.MESH
N_CTX = 32


def scan_kernel(backward, s_ref, dec_ref, out_ref, got_dec, got, pre, send_a, recv_a, send_d, recv_d, send_b, recv_b, own_sem):
    me = lax.axis_index("ctx")
    barrier = pltpu.get_barrier_semaphore()

    def peer_of(k):
        return lax.rem(me + k, N_CTX)

    def greet(k, c):
        pl.semaphore_signal(barrier, inc=1, device_id={"ctx": peer_of(k)}, device_id_type=MESH)
        return c

    lax.fori_loop(1, N_CTX, greet, 0)
    pl.semaphore_wait(barrier, N_CTX - 1)

    def copy_a(k):
        return pltpu.make_async_remote_copy(
            src_ref=s_ref.at[peer_of(k)], dst_ref=got.at[me],
            send_sem=send_a.at[k], recv_sem=recv_a.at[k],
            device_id={"ctx": peer_of(k)}, device_id_type=MESH)

    def copy_d(k):
        return pltpu.make_async_remote_copy(
            src_ref=dec_ref.at[peer_of(k)], dst_ref=got_dec.at[me],
            send_sem=send_d.at[k], recv_sem=recv_d.at[k],
            device_id={"ctx": peer_of(k)}, device_id_type=MESH)

    def copy_b(k):
        return pltpu.make_async_remote_copy(
            src_ref=pre.at[peer_of(k)], dst_ref=out_ref.at[me],
            send_sem=send_b.at[k], recv_sem=recv_b.at[k],
            device_id={"ctx": peer_of(k)}, device_id_type=MESH)

    def start(make):
        def step(k, c):
            make(k).start()
            return c
        lax.fori_loop(1, N_CTX, step, 0)

    def finish(make):
        def step(k, c):
            make(k).wait()
            return c
        lax.fori_loop(1, N_CTX, step, 0)

    if not backward:
        start(copy_d)
    start(copy_a)
    own = pltpu.make_async_copy(s_ref.at[me], got.at[me], own_sem.at[0])
    own.start()
    if not backward:
        own_d = pltpu.make_async_copy(dec_ref.at[me], got_dec.at[me], own_sem.at[1])
        own_d.start()
        own_d.wait()
        finish(copy_d)
    own.wait()
    finish(copy_a)

    decays = dec_ref if backward else got_dec

    def fold(i, carry):
        first, second = carry
        at = N_CTX - 1 - i if backward else i
        pre[at, 0:64, :] = first.astype(jnp.bfloat16)
        pre[at, 64:128, :] = second.astype(jnp.bfloat16)
        first = decays[at, 0:1, :] * first + got[at, 0:64, :].astype(jnp.float32)
        second = decays[at, 8:9, :] * second + got[at, 64:128, :].astype(jnp.float32)
        return (first, second)

    zero = jnp.zeros((64, 128), jnp.float32)
    lax.fori_loop(0, N_CTX, fold, (zero, zero))

    start(copy_b)
    own_b = pltpu.make_async_copy(pre.at[me], out_ref.at[me], own_sem.at[2])
    own_b.start()
    own_b.wait()
    finish(copy_b)


def state_scan(summary, decay, backward):
    vmem = pl.BlockSpec(memory_space=pltpu.VMEM)
    dma = pltpu.SemaphoreType.DMA
    bf = jax.ShapeDtypeStruct((N_CTX, 128, 128), jnp.bfloat16)
    dec = jax.ShapeDtypeStruct((N_CTX, 16, 128), jnp.float32)
    scratch = [
        pltpu.VMEM((N_CTX, 128, 128), jnp.bfloat16),
        pltpu.VMEM((N_CTX, 128, 128), jnp.bfloat16),
        dma((N_CTX,)), dma((N_CTX,)), dma((N_CTX,)), dma((N_CTX,)), dma((N_CTX,)), dma((N_CTX,)),
        dma((3,)),
    ]
    params = pltpu.CompilerParams(collective_id=2 if backward else 1, has_side_effects=True)
    cost = pl.CostEstimate(flops=1000000, bytes_accessed=4000000, transcendentals=0)
    if backward:
        def kernel(s_ref, dec_ref, out_ref, *rest):
            scan_kernel(True, s_ref, dec_ref, out_ref, None, *rest)
        return pl.pallas_call(
            kernel, out_shape=bf, in_specs=[vmem, vmem], out_specs=vmem,
            scratch_shapes=scratch, compiler_params=params, cost_estimate=cost, name="scan_bwd")(summary, decay)
    return pl.pallas_call(
        functools.partial(scan_kernel, False), out_shape=(bf, dec), in_specs=[vmem, vmem], out_specs=(vmem, vmem),
        scratch_shapes=scratch, compiler_params=params, cost_estimate=cost, name="scan_fwd")(summary, decay)


CUTS = ((0, 768), (768, 1408), (1408, 2048))


def scatter_kernel(s_ref, out_ref, *scratch):
    (ra0, ra1, ra2, sa0, sa1, sa2, rb0, rb1, rb2, sb0, sb1, sb2, rc0, rc1, rc2, send_sem, recv_sem) = scratch
    dp, ctx = lax.axis_index("dp"), lax.axis_index("ctx")
    x_lo, core = dp // 2, lax.rem(dp, 2)
    x_hi, z, y = ctx // 16, lax.rem(ctx // 4, 4), lax.rem(ctx, 4)
    at = {"x": x_lo * 2 + x_hi, "z": z, "y": y}

    def peer(axis, k):
        there = lax.rem(at[axis] + k, 4)
        if axis == "y":
            return there, (dp, x_hi * 16 + z * 4 + there)
        if axis == "z":
            return there, (dp, x_hi * 16 + there * 4 + y)
        return there, ((there // 2) * 2 + core, lax.rem(there, 2) * 16 + z * 4 + y)

    barrier = pltpu.get_barrier_semaphore()
    for axis in "yzx":
        for k in (1, 2, 3):
            pl.semaphore_signal(barrier, inc=1, device_id=peer(axis, k)[1], device_id_type=MESH)
    pl.semaphore_wait(barrier, 9)

    def send(stage, part, k, axis, pick, dst):
        there, device = peer(axis, k)
        index = (stage * 3 + part) * 3 + k - 1
        copy = pltpu.make_async_remote_copy(
            src_ref=pick(there), dst_ref=dst.at[k - 1],
            send_sem=send_sem.at[index], recv_sem=recv_sem.at[index],
            device_id=device, device_id_type=MESH)
        copy.start()
        return copy

    cols = [pl.ds(a, b - a) for a, b in CUTS]
    picks_a = (
        lambda t: s_ref.at[:, :, t, :, cols[0]],
        lambda t: s_ref.at[:, t, :, :, cols[1]],
        lambda t: s_ref.at[t, :, :, :, cols[2]],
    )
    axes = (("y", "z", "x"), ("z", "x", "y"), ("x", "y", "z"))
    first = [[send(0, p, k, axes[p][0], picks_a[p], (ra0, ra1, ra2)[p]) for k in (2, 1, 3)] for p in range(3)]

    def add(mine, recv, i):
        total = mine.astype(jnp.float32)
        for k in range(3):
            total = total + recv[(k,) + i].astype(jnp.float32)
        return total

    second = []
    for p in range(3):
        for copy in first[p]:
            copy.wait()
        ra, sa = (ra0, ra1, ra2)[p], (sa0, sa1, sa2)[p]

        def body(i, c, p=p, ra=ra, sa=sa):
            a, b = i // 4, lax.rem(i, 4)
            if p == 0:
                mine = s_ref[a, b, y, :, cols[0]]
            elif p == 1:
                mine = s_ref[a, z, b, :, cols[1]]
            else:
                mine = s_ref[at["x"], a, b, :, cols[2]]
            sa[a, b] = add(mine, ra, (a, b)).astype(jnp.bfloat16)
            return c

        lax.fori_loop(0, 16, body, 0)
        pick = (lambda t: sa0.at[:, t], lambda t: sa1.at[t], lambda t: sa2.at[:, t])[p]
        second.append([send(1, p, k, axes[p][1], pick, (rb0, rb1, rb2)[p]) for k in (2, 1, 3)])
    third = []
    for p in range(3):
        for copy in second[p]:
            copy.wait()
        sa, rb, sb = (sa0, sa1, sa2)[p], (rb0, rb1, rb2)[p], (sb0, sb1, sb2)[p]
        for i in range(4):
            mine = (lambda: sa0[i, z], lambda: sa1[at["x"], i], lambda: sa2[i, y])[p]()
            sb[i] = add(mine, rb, (i,)).astype(jnp.bfloat16)
        third.append([send(2, p, k, axes[p][2], lambda t, sb=sb: sb.at[t], (rc0, rc1, rc2)[p]) for k in (2, 1, 3)])
    for p in range(3):
        for copy in third[p]:
            copy.wait()
        sb, rc = (sb0, sb1, sb2)[p], (rc0, rc1, rc2)[p]
        out_ref[:, cols[p]] = add(sb[at[axes[p][2]]], rc, ())


def weight_scatter(partial):
    vmem = pl.BlockSpec(memory_space=pltpu.VMEM)
    widths = [b - a for a, b in CUTS]
    bf = jnp.bfloat16
    scratch = [pltpu.VMEM((3, 4, 4, 16, w), bf) for w in widths]
    scratch += [pltpu.VMEM((4, 4, 16, w), bf) for w in widths]
    scratch += [pltpu.VMEM((3, 4, 16, w), bf) for w in widths]
    scratch += [pltpu.VMEM((4, 16, w), bf) for w in widths]
    scratch += [pltpu.VMEM((3, 16, w), bf) for w in widths]
    scratch += [pltpu.SemaphoreType.DMA((27,)), pltpu.SemaphoreType.DMA((27,))]
    return pl.pallas_call(
        scatter_kernel, out_shape=jax.ShapeDtypeStruct((16, 2048), jnp.float32),
        in_specs=[vmem], out_specs=vmem, scratch_shapes=scratch,
        compiler_params=pltpu.CompilerParams(collective_id=3, has_side_effects=True),
        cost_estimate=pl.CostEstimate(flops=1000000, bytes_accessed=8000000, transcendentals=0),
        name="weight_scatter")(partial)


def sum_kernel(v_ref, out_ref, plane, line, part, send_a, recv_a, send_b, recv_b, own_sem):
    dp, ctx = lax.axis_index("dp"), lax.axis_index("ctx")
    q, x_hi = lax.rem(ctx, 16), ctx // 16
    e = x_hi * 4 + dp

    def peer_a(k):
        return (dp, x_hi * 16 + lax.rem(q + k, 16))

    def peer_b(k):
        there = lax.rem(e + k, 8)
        return (lax.rem(there, 4), (there // 4) * 16 + q)

    barrier = pltpu.get_barrier_semaphore()
    for k in range(1, 16):
        pl.semaphore_signal(barrier, inc=1, device_id=peer_a(k), device_id_type=MESH)
    for k in range(1, 8):
        pl.semaphore_signal(barrier, inc=1, device_id=peer_b(k), device_id_type=MESH)
    pl.semaphore_wait(barrier, 22)

    def copy_a(k):
        return pltpu.make_async_remote_copy(
            src_ref=v_ref, dst_ref=plane.at[q], send_sem=send_a.at[k], recv_sem=recv_a.at[k],
            device_id=peer_a(k), device_id_type=MESH)

    def copy_b(k):
        return pltpu.make_async_remote_copy(
            src_ref=part, dst_ref=line.at[e], send_sem=send_b.at[k], recv_sem=recv_b.at[k],
            device_id=peer_b(k), device_id_type=MESH)

    first = [copy_a(k) for k in range(1, 16)]
    for copy in first:
        copy.start()
    plane[q] = v_ref[...]
    for copy in first:
        copy.wait()
    total = plane[0]
    for i in range(1, 16):
        total = total + plane[i]
    part[...] = total
    second = [copy_b(k) for k in range(1, 8)]
    for copy in second:
        copy.start()
    line[e] = total
    for copy in second:
        copy.wait()
    total = line[0]
    for i in range(1, 8):
        total = total + line[i]
    out_ref[...] = total


def small_sum(value):
    vmem = pl.BlockSpec(memory_space=pltpu.VMEM)
    dma = pltpu.SemaphoreType.DMA
    shape = value.shape
    return pl.pallas_call(
        sum_kernel, out_shape=jax.ShapeDtypeStruct(shape, jnp.float32), in_specs=[vmem], out_specs=vmem,
        scratch_shapes=[
            pltpu.VMEM((16,) + shape, jnp.float32), pltpu.VMEM((8,) + shape, jnp.float32),
            pltpu.VMEM(shape, jnp.float32), dma((16,)), dma((16,)), dma((8,)), dma((8,)), dma((1,))],
        compiler_params=pltpu.CompilerParams(collective_id=4, has_side_effects=True),
        cost_estimate=pl.CostEstimate(flops=100000, bytes_accessed=400000, transcendentals=0),
        name="small_sum")(value)

H = 32
P_SIZE = 64
NS = 128
DI = 2048
Q = 128
PAIRS = 16
B_AT = 2 * DI
C_AT = 2 * DI + NS
bf16 = jnp.bfloat16
f32 = jnp.float32
precise = lax.Precision.HIGHEST


def dot(a, b, dims=((1,), (0,)), precision=None):
    return lax.dot_general(a, b, (dims, ((), ())), precision=precision, preferred_element_type=f32)


ROWS = ((0,), (0,))
LANES = ((1,), (1,))


def iota(shape, axis):
    return lax.broadcasted_iota(jnp.int32, shape, axis)


def head_map():
    return (iota((H, DI), 0) == iota((H, DI), 1) // P_SIZE).astype(f32).astype(bf16)


def expand(value, heads):
    high = value.astype(bf16)
    low = (value - high.astype(f32)).astype(bf16)
    return dot(high, heads) + dot(low, heads)


def per_head(value, heads):
    return dot(value.astype(bf16), heads, LANES)


def softplus(value):
    return jnp.maximum(value, 0.0) + jnp.log1p(jnp.exp(-jnp.abs(value)))


def sigmoid(value):
    return 1.0 / (1.0 + jnp.exp(-value))


def tril():
    return iota((Q, Q), 0) >= iota((Q, Q), 1)


def half_masks():
    left = (iota((Q, 128), 1) < P_SIZE).astype(f32)
    return left.astype(bf16), (1.0 - left).astype(bf16)


def summary_kernel(proj, dt_raw, dt_raw_t, rate, bias, rate_t, bias_t, state, decay, dt_out, run_out, dt_t_out, run_t_out):
    lower = tril().astype(f32)
    dt = softplus(dt_raw[0].astype(f32) + bias[...])
    run = dot(lower, -rate[...] * dt, precision=precise)
    dt_t = softplus(dt_raw_t[0].astype(f32) + bias_t[...])
    run_t = dot(-rate_t[...] * dt_t, lower, LANES, precision=precise)
    dt_out[0] = dt
    run_out[0] = run
    dt_t_out[0] = dt_t
    run_t_out[0] = run_t
    weight = jnp.exp(run[Q - 1 : Q, :] - run) * dt
    weighed = (expand(weight, head_map()) * proj[0, :, DI:B_AT].astype(f32)).astype(bf16)
    total = dot(weighed, proj[0, :, B_AT:C_AT], ROWS)
    state[...] = total.astype(bf16).reshape(H, P_SIZE, NS)
    left = jnp.exp(run_t[:, Q - 1 : Q])
    for h in range(H):
        decay[h] = jnp.broadcast_to(left[h : h + 1, :], (8, 128))


def forward_kernel(proj, dt_raw_unused, run, dt_t, run_t, entering, skip, gain, normed, y_out, spread_out, mix_out, local):
    write, read = proj[0, :, B_AT:C_AT], proj[0, :, C_AT:]
    affinity = dot(read, write, LANES)
    affinity = jnp.concatenate([affinity, affinity], 1)
    causal = tril()
    left, right = half_masks()
    for j in range(PAIRS):
        cols = slice(DI + 128 * j, DI + 128 * j + 128)
        both = []
        for h in (2 * j, 2 * j + 1):
            gap = run[0, :, h : h + 1] - run_t[0, h : h + 1, :]
            both.append(jnp.exp(jnp.where(causal, gap, -1e30)) * dt_t[0, h : h + 1, :])
        spread = jnp.concatenate(both, 1)
        spread_out[0, j] = spread.astype(bf16)
        values = proj[0, :, cols]
        stacked = jnp.concatenate([values * left, values * right], 0)
        mixing = (spread * affinity).astype(bf16)
        mix_out[0, j] = mixing
        local[:, 128 * j : 128 * j + 128] = dot(mixing, stacked)
    carried = dot(read, entering[...].reshape(DI, NS), LANES)
    grown = expand(jnp.exp(run[0]), head_map())
    y = local[...] + grown * carried + skip[...] * proj[0, :, DI:B_AT].astype(f32)
    y_out[0] = y
    gate = proj[0, :, :DI].astype(f32)
    gated = y * gate * sigmoid(gate)
    inv = lax.rsqrt(jnp.mean(gated * gated, axis=1, keepdims=True) + 1e-05)
    normed[0] = (gated * inv * gain[...]).astype(bf16)


def backward_kernel(proj, y_in, d_normed, run, spread_in, mix_in, entering, skip, gain,
                    d_gate, d_x, d_entering, d_write, d_read, gains, from_y, from_x, dy_keep, dx_keep):
    heads = head_map()
    gate = proj[0, :, :DI].astype(f32)
    y = y_in[0]
    sig = sigmoid(gate)
    silu = gate * sig
    gated = y * silu
    inv = lax.rsqrt(jnp.mean(gated * gated, axis=1, keepdims=True) + 1e-05)
    dn = d_normed[0].astype(f32)
    gains[0, 0:1, :] = jnp.sum(dn * (gated * inv), axis=0, keepdims=True)
    up = dn * gain[...]
    pull = jnp.mean(up * gated, axis=1, keepdims=True) * (inv * inv * inv)
    d_gated = inv * up - gated * pull
    dy = d_gated * silu
    d_gate[0] = (d_gated * y * (sig * (1.0 + gate * (1.0 - sig)))).astype(bf16)
    values = proj[0, :, DI:B_AT].astype(f32)
    gains[0, 1:2, :] = jnp.sum(dy * values, axis=0, keepdims=True)
    dy_keep[...] = dy.astype(bf16)
    from_y[0] = per_head(dy_keep[...].astype(f32) * (y - skip[...] * values), heads)
    grown = (expand(jnp.exp(run[0]), heads) * dy).astype(bf16)
    write, read = proj[0, :, B_AT:C_AT], proj[0, :, C_AT:]
    state = entering[...].reshape(DI, NS)
    d_entering[...] = dot(grown, read, ROWS).astype(bf16).reshape(H, P_SIZE, NS)
    d_c = dot(grown, state)
    left, right = half_masks()
    first = iota((Q, 128), 1) < P_SIZE
    d_aff = jnp.zeros((Q, Q), f32)
    for j in range(PAIRS):
        cols = slice(128 * j, 128 * j + 128)
        dyp = dy_keep[:, cols]
        x = proj[0, :, DI + 128 * j : DI + 128 * j + 128]
        stacked = jnp.concatenate([x * left, x * right], 0)
        d_mix = dot(dyp, stacked, LANES) * spread_in[0, j].astype(f32)
        d_aff = d_aff + d_mix[:, :Q] + d_mix[:, Q:]
        back = dot(mix_in[0, j], dyp, ROWS)
        dx_keep[:, cols] = jnp.where(first, back[:Q], back[Q:])
    d_aff = d_aff.astype(bf16)
    d_read[0] = (d_c + dot(d_aff, write)).astype(bf16)
    d_write[0] = dot(d_aff, read, ROWS)
    dx = dx_keep[...]
    from_x[0] = per_head(values * dx, heads)
    d_x[0] = dx + skip[...] * dy


def finish_kernel(proj, dt_raw, dt_in, run_in, leaving, entering, from_y, from_x, d_x, d_gate, d_write, d_read,
                  rate, bias, d_proj, d_dt, sums):
    heads = head_map()
    dt, run = dt_in[0], run_in[0]
    last = run[Q - 1 : Q, :]
    weight = expand(jnp.exp(last - run) * dt, heads)
    values = proj[0, :, DI:B_AT].astype(f32)
    out = leaving[...].reshape(DI, NS)
    d_state = weight * dot(proj[0, :, B_AT:C_AT], out, LANES)
    d_b = d_write[0] + dot((weight * values).astype(bf16), out)
    d_proj[0, :, :DI] = d_gate[0]
    d_proj[0, :, DI:B_AT] = (d_x[0] + d_state).astype(bf16)
    d_proj[0, :, B_AT:C_AT] = d_b.astype(bf16)
    d_proj[0, :, C_AT:] = d_read[0]
    from_state = per_head(values * d_state, heads)
    total = from_x[0] + from_state
    meet = jnp.sum(entering[...].astype(f32) * leaving[...].astype(f32), axis=1)
    meet = dot(jnp.ones((8, NS), f32), meet, LANES, precision=precise)[0:1, :]
    d_last = jnp.exp(last) * meet + jnp.sum(from_state, axis=0, keepdims=True)
    upper = (iota((Q, Q), 0) <= iota((Q, Q), 1)).astype(f32)
    d_log = dot(upper, from_y[0] - total, precision=precise) + d_last
    d_step = total / dt - rate[...] * d_log
    d_raw = d_step * sigmoid(dt_raw[0].astype(f32) + bias[...])
    d_dt[0] = d_raw.astype(bf16)
    sums[0, 0:1, :] = jnp.sum(d_log * (-rate[...] * dt), axis=0, keepdims=True)
    sums[0, 1:2, :] = jnp.sum(d_raw, axis=0, keepdims=True)


def strand(*shape):
    return pl.BlockSpec((1,) + shape, lambda s: (s,) + (0,) * len(shape))


def shared(*shape):
    return pl.BlockSpec(shape, lambda s: (0,) * len(shape))


STATE = pl.BlockSpec((H, P_SIZE, NS), lambda s: (0, s, 0))


def like(dtype, *shape):
    return jax.ShapeDtypeStruct(shape, dtype)


def strand_call(kernel, name, in_specs, out_specs, out_shape, scratch=(), flops=2000000000):
    return pl.pallas_call(
        kernel, grid=(2,), in_specs=in_specs, out_specs=out_specs, out_shape=out_shape,
        scratch_shapes=list(scratch), name=name,
        cost_estimate=pl.CostEstimate(flops=flops, bytes_accessed=10000000, transcendentals=0))


def flipped(block):
    turn = (iota((128, 128), 0) + iota((128, 128), 1) == 127).astype(f32).astype(bf16)
    rows = dot(turn, block).astype(bf16)
    parts = [dot(rows[:, 128 * j : 128 * j + 128], turn) for j in range(15, -1, -1)]
    return jnp.concatenate(parts, 1)


def flip_kernel(keep, got, out):
    out[0] = keep[...]
    out[1] = flipped(got[...]).astype(bf16)


def mix_kernel(own, got, out):
    out[...] = (own[...].astype(f32) + flipped(got[...])).astype(bf16)


def whole_call(kernel, name, out_shape, *args):
    vmem = pl.BlockSpec(memory_space=pltpu.VMEM)
    return pl.pallas_call(
        kernel, out_shape=out_shape, in_specs=[vmem] * len(args), out_specs=vmem, name=name,
        cost_estimate=pl.CostEstimate(flops=200000000, bytes_accessed=2000000, transcendentals=0))(*args)


def mirror(value):
    return lax.ppermute(value, "ctx", [(i, N_CTX - 1 - i) for i in range(N_CTX)])


def weight_grad(grads, normed):
    core = lax.rem(lax.axis_index("dp"), 2)
    swap = [(i, i ^ 1) for i in range(4)]
    parts = grads.reshape(256, 2, 2, 512)
    mine = lax.dynamic_index_in_dim(parts, core, 2, keepdims=False).reshape(256, 1024)
    theirs = lax.dynamic_index_in_dim(parts, 1 - core, 2, keepdims=False).reshape(256, 1024)
    grads_two = jnp.concatenate([mine, lax.ppermute(theirs, "dp", swap)], 0)
    normed_two = jnp.concatenate([normed, lax.ppermute(normed, "dp", swap)], 0)
    partial = lax.dot_general(
        grads_two, normed_two, (((0,), (0,)), ((), ())), preferred_element_type=f32
    ).astype(bf16)
    return weight_scatter(partial.reshape(4, 4, 4, 16, DI))


def body(projections, dt_raw, a_log, dt_bias, skip_gain, norm_gain, w_out, base_ids, cotangent):
    keep = cotangent * (base_ids != 4).astype(bf16)[:, None]
    d_out = whole_call(flip_kernel, "flip_keep", like(bf16, 2, Q, DI), keep, mirror(keep))
    rate = jnp.exp(a_log)
    proj, tok = strand(Q, 2 * DI + 2 * NS), strand(Q, H)
    tok_t, wide = strand(H, Q), strand(Q, DI)
    row, col, lane = shared(1, H), shared(H, 1), shared(1, DI)
    skip, gain = jnp.repeat(skip_gain, P_SIZE)[None], norm_gain[None]
    state, factor, dt, run, dt_t, run_t = strand_call(
        summary_kernel, "summary", [proj, tok, tok_t, row, row, col, col],
        [STATE, pl.BlockSpec((H, 8, NS), lambda s: (0, s, 0)), tok, tok, tok_t, tok_t],
        [like(bf16, H, 2 * P_SIZE, NS), like(f32, H, 16, NS), like(f32, 2, Q, H), like(f32, 2, Q, H),
         like(f32, 2, H, Q), like(f32, 2, H, Q)],
    )(projections, dt_raw, jnp.swapaxes(dt_raw, 1, 2), rate[None], dt_bias[None], rate[:, None], dt_bias[:, None])
    entering, decays = state_scan(state, factor, False)
    spread_spec = strand(PAIRS, Q, 2 * Q)
    normed, y, spread, mixing = strand_call(
        forward_kernel, "forward", [proj, tok, tok, tok_t, tok_t, STATE, lane, lane],
        [wide, wide, spread_spec, spread_spec],
        [like(bf16, 2, Q, DI), like(f32, 2, Q, DI), like(bf16, 2, PAIRS, Q, 2 * Q),
         like(bf16, 2, PAIRS, Q, 2 * Q)],
        [pltpu.VMEM((Q, DI), f32)],
    )(projections, dt_raw, run, dt_t, run_t, entering, skip, gain)
    strand_out = jnp.einsum("srk,dk->srd", normed, w_out, preferred_element_type=f32).astype(bf16)
    moved = mirror(strand_out[1])
    d_normed = jnp.einsum("srd,dk->srk", d_out, w_out, preferred_element_type=f32).astype(bf16)
    d_gate, d_x, d_entering, d_write, d_read, gains, from_y, from_x = strand_call(
        backward_kernel, "backward", [proj, wide, wide, tok, spread_spec, spread_spec, STATE, lane, lane],
        [wide, wide, STATE, strand(Q, NS), strand(Q, NS), strand(2, DI), tok, tok],
        [like(bf16, 2, Q, DI), like(f32, 2, Q, DI), like(bf16, H, 2 * P_SIZE, NS), like(f32, 2, Q, NS),
         like(bf16, 2, Q, NS), like(f32, 2, 2, DI), like(f32, 2, Q, H), like(f32, 2, Q, H)],
        [pltpu.VMEM((Q, DI), bf16), pltpu.VMEM((Q, DI), f32)],
    )(projections, y, d_normed, run, spread, mixing, entering, skip, gain)
    leaving = state_scan(d_entering, decays, True)
    d_w_out = weight_grad(d_out.reshape(2 * Q, DI), normed.reshape(2 * Q, DI))
    mixed_out = whole_call(mix_kernel, "mix", like(bf16, Q, DI), strand_out[0], moved)
    d_proj, d_dt, sums = strand_call(
        finish_kernel, "finish",
        [proj, tok, tok, tok, STATE, STATE, tok, tok, wide, wide, strand(Q, NS), strand(Q, NS), row, row],
        [proj, tok, strand(2, H)],
        [like(bf16, 2, Q, 2 * DI + 2 * NS), like(bf16, 2, Q, H), like(f32, 2, 2, H)],
    )(projections, dt_raw, dt, run, leaving, entering, from_y, from_x, d_x, d_gate, d_write, d_read,
      rate[None], dt_bias[None])
    gains = jnp.sum(gains, axis=0)
    d_skip = jnp.sum(gains[1].reshape(H, P_SIZE), axis=1)
    small = jnp.concatenate([gains[0], jnp.sum(sums, axis=0).reshape(-1), d_skip, jnp.zeros((928,), f32)])
    summed = small_sum(small.reshape(24, 128)).reshape(-1)
    return (mixed_out, d_proj, d_dt, d_w_out, summed[2048 : 2048 + 96].reshape(3, 32), summed[:2048])


def solution(mesh):
    placed = (
        P(None, ("dp", "ctx"), None),
        P(None, ("dp", "ctx"), None),
        P(),
        P(),
        P(),
        P(),
        P(),
        P(("dp", "ctx")),
        P(("dp", "ctx"), None),
    )
    return jax.shard_map(
        body,
        mesh=mesh,
        in_specs=placed,
        out_specs=(
            P(("dp", "ctx"), None),
            P(None, ("dp", "ctx"), None),
            P(None, ("dp", "ctx"), None),
            P(("dp", "ctx"), None),
            P(),
            P(),
        ),
        check_vma=False,
    )
```

profile of v0, /device:TPU:4, one launch (start us, length us, event | category | flops | bytes accessed | tf_op | source)
XLA Modules:
  0.0 218.1 jit_solution(13774487594398232866)
XLA Ops:
  0.6 0.7 compare_convert_fusion
  1.3 1.1 broadcast_multiply_fusion.keep
  2.4 0.0 copy-start.1
  2.5 6.5 %collective-permute-start.1 = (bf16[128,2048]{1,0:T(8,128)(2,1)S(1)}, bf16[128,2048]{1,0:T(8,128)(2,1)S(1)}, u32[]{:S(2)}, u32[]{:S(2)}) collective-permute-start(bf16[128,2048]{1,0:T(8,128)(2,1)S(1)} %broadcast_multiply_fusion.keep), channel_id=1, source_target_pairs={{0,31},{1,30},{2,29},{3,28},{4,27},{5,26},{6,25},{7,24},{8,23},{9,... | collective-permute-start | bytes 1572872 | tf_op jit(solution)/shard_map/ppermute | solution.py:506
  9.0 1.4 copy.32.dt_raw.dt_raw_unused
  10.4 1.3 exponential_bitcast_fusion
  11.7 0.7 copy.30.rate_t
  12.4 1.3 copy.31.bias_t
  13.7 0.7 broadcast_in_dim.28
  14.4 0.7 broadcast_in_dim_reshape.3.skip
  15.1 4.3 %summary.1 = (bf16[32,128,128]{2,1,0:T(8,128)(2,1)}, f32[32,16,128]{2,1,0:T(8,128)}, f32[2,128,32]{2,1,0:T(8,128)}, f32[2,128,32]{2,1,0:T(8,128)}, f32[2,32,128]{2,1,0:T(8,128)}, /*index=5*/f32[2,32,128]{2,1,0:T(8,128)}) custom-call(bf16[2,128,4352]{2,1,0:T(8,128)(2,1)} %proj.7, bf16[2,128,32]{2,1,0:T(8,128)(2,1)} %copy.32.dt_raw.dt_raw_unused, ...), custom_call_target="tpu_custom_call" | custom-call | flops 2000000000 | bytes 10000000 | tf_op jit(solution)/shard_map/summary/pallas_call | solution.py:531
  19.4 0.0 copy-done.1
  19.4 39.7 %scan_fwd.1 = (bf16[32,128,128]{2,1,0:T(8,128)(2,1)}, f32[32,16,128]{2,1,0:T(8,128)}) custom-call(bf16[32,128,128]{2,1,0:T(8,128)(2,1)} %get-tuple-element.32.s_ref, f32[32,16,128]{2,1,0:T(8,128)} %get-tuple-element.33.dec_ref), custom_call_target="tpu_custom_call" | custom-call | flops 1000000 | bytes 4000000 | tf_op jit(solution)/shard_map/scan_fwd/pallas_call | solution.py:111
  59.1 7.1 %forward.1 = (bf16[2,128,2048]{2,1,0:T(8,128)(2,1)}, f32[2,128,2048]{2,1,0:T(8,128)}, bf16[2,16,128,256]{3,2,1,0:T(8,128)(2,1)}, bf16[2,16,128,256]{3,2,1,0:T(8,128)(2,1)}) custom-call(bf16[2,128,4352]{2,1,0:T(8,128)(2,1)} %proj.7, bf16[2,128,32]{2,1,0:T(8,128)(2,1)} %copy.32.dt_raw.dt_raw_unused, f32[2,128,32]{2,1,0:T(8,128)} %get-tuple-element.29.run.run_in, ...), custom_call_target="tpu_custom_call" | custom-call | flops 2000000000 | bytes 10000000 | tf_op jit(solution)/shard_map/forward/pallas_call | solution.py:539
  66.2 0.1 collective-permute-start.3
  66.3 6.1 %fusion.4 = bf16[2,128,2048]{2,1,0:T(8,128)(2,1)S(1)} fusion(bf16[2,128,2048]{2,1,0:T(8,128)(2,1)} %get-tuple-element.35, bf16[2048,2048]{1,0:T(8,128)(2,1)} %param.15), kind=kOutput, calls=%fused_computation.5 | convolution fusion | flops 2148007936 | bytes 10485760 | tf_op jit(solution)/shard_map/srk,dk->srd/dot_general | solution.py:546
  72.4 1.1 slice_bitcast_fusion
  73.5 8.0 %collective-permute-start = (bf16[128,2048]{1,0:T(8,128)(2,1)}, bf16[128,2048]{1,0:T(8,128)(2,1)}, u32[]{:S(2)}, u32[]{:S(2)}) collective-permute-start(bf16[128,2048]{1,0:T(8,128)(2,1)} %get-tuple-element.72), channel_id=1, source_target_pairs={{0,31},{1,30},{2,29},{3,28},{4,27},{5,26},{6,25},{7,24},{8,23},{9,... | collective-permute-start | bytes 1572872 | tf_op jit(solution)/shard_map/ppermute | solution.py:506
  81.5 0.0 collective-permute-done.1.got
  81.5 0.0 copy-start.2
  81.5 0.8 copy-done.2
  82.3 2.7 %flip_keep.1 = bf16[2,128,2048]{2,1,0:T(8,128)(2,1)} custom-call(bf16[128,2048]{1,0:T(8,128)(2,1)} %copy-done.1, bf16[128,2048]{1,0:T(8,128)(2,1)} %copy-done.2), custom_call_target="tpu_custom_call" | custom-call | flops 200000000 | bytes 2000000 | tf_op jit(solution)/shard_map/flip_keep/pallas_call | solution.py:500
  85.0 0.0 copy-start
  85.0 7.1 %fusion.7.d_normed = bf16[2,128,2048]{2,1,0:T(8,128)(2,1)} fusion(bf16[2,128,2048]{2,1,0:T(8,128)(2,1)} %flip_keep.1, bf16[2048,2048]{1,0:T(8,128)(2,1)} %param.15), kind=kOutput, calls=%fused_computation.6 | convolution fusion | flops 2148007936 | bytes 10485760 | tf_op jit(solution)/shard_map/srd,dk->srk/dot_general | solution.py:548
  92.2 0.0 copy-done
  92.2 0.8 reshape_reshape.3
  93.0 2.2 constant_dynamic-slice_fusion.1
  95.1 0.9 copy.38
  96.1 0.5 collective-permute-start.2
  96.5 9.2 %backward.1 = (bf16[2,128,2048]{2,1,0:T(8,128)(2,1)}, f32[2,128,2048]{2,1,0:T(8,128)}, bf16[32,128,128]{2,1,0:T(8,128)(2,1)}, f32[2,128,128]{2,1,0:T(8,128)}, bf...) custom-call(bf16[2,128,4352]{2,1,0:T(8,128)(2,1)} %proj.7, ...), custom_call_target="tpu_custom_call" | custom-call | flops 2000000000 | bytes 10000000 | tf_op jit(solution)/shard_map/backward/pallas_call | solution.py:549
  105.8 37.0 %scan_bwd.1.leaving = bf16[32,128,128]{2,1,0:T(8,128)(2,1)} custom-call(bf16[32,128,128]{2,1,0:T(8,128)(2,1)} %get-tuple-element.40.s_ref, f32[32,16,128]{2,1,0:T(8,128)} %get-tuple-element.41.dec_ref), custom_call_target="tpu_custom_call" | custom-call | flops 1000000 | bytes 4000000 | tf_op jit(solution)/shard_map/scan_bwd/pallas_call | solution.py:108
  142.8 0.0 copy-start.4
  142.8 5.6 %finish.1 = (bf16[2,128,4352]{2,1,0:T(8,128)(2,1)}, bf16[2,128,32]{2,1,0:T(8,128)(2,1)}, f32[2,2,32]{2,1,0:T(2,128)}) custom-call(bf16[2,128,4352]{2,1,0:T(8,128)(2,1)} %proj.7, bf16[2,128,32]{2,1,0:T(8,128)(2,1)} %copy.32.dt_raw.dt_raw_unused, f32[2,128,32]{2,1,0:T(8,128)} %get-tuple-element.36.dt_in, f32[2,128,32]{2,1,0:T(8,128)} %get-tuple-element.29.run.run_in, ...), custom_call_target="tpu_custom_call" | custom-call | flops 2000000000 | bytes 10000000 | tf_op jit(solution)/shard_map/finish/pallas_call | solution.py:559
  148.5 0.7 reduce_sum.28
  149.2 0.1 reshape.42
  149.2 0.0 copy-done.4
  149.3 0.1 reshape_squeeze.3
  149.4 0.1 reduce_sum.29
  149.5 0.7 concatenate.11
  150.2 17.8 %small_sum.1 = f32[24,128]{1,0:T(8,128)} custom-call(f32[24,128]{1,0:T(8,128)} %bitcast.34), custom_call_target="tpu_custom_call" | custom-call | flops 100000 | bytes 400000 | tf_op jit(solution)/shard_map/small_sum/pallas_call | solution.py:274
  167.9 0.0 copy-start.3
  168.0 0.8 slice.28
  168.8 0.6 slice.36
  169.4 0.9 copy.37
  170.3 1.5 copy.36
  171.8 0.0 collective-permute-done.got
  171.8 2.5 %mix.1 = bf16[128,2048]{1,0:T(8,128)(2,1)} custom-call(bf16[128,2048]{1,0:T(8,128)(2,1)} %get-tuple-element.73.own, bf16[128,2048]{1,0:T(8,128)(2,1)} %collective-permute-done.got), custom_call_target="tpu_custom_call" | custom-call | flops 200000000 | bytes 2000000 | tf_op jit(solution)/shard_map/mix/pallas_call | solution.py:500
  174.4 0.0 copy-done.3
  174.4 0.6 slice_bitcast_fusion.2
  175.0 0.0 collective-permute-done.2
  175.0 0.0 collective-permute-done.3
  175.0 5.8 %convolution_convert_fusion = bf16[1024,2048]{1,0:T(8,128)(2,1)} fusion(bf16[256,2048]{1,0:T(8,128)(2,1)} %collective-permute-done.3, bf16[256,2048]{1,0:T(8,128)(2,1)} %bitcast.43, bf16[256,1024]{0,1:T(8,128)(2,1)S(1)} %collective-permute-done.2, bf16[256,1024]{0,1:T(8,128)(2,1)S(1)} %bitcast.33), kind=kOutput, calls=%fused_computation.4 | convolution fusion | flops 2155872256 | bytes 7340032 | tf_op jit(solution)/shard_map/dot_general | solution.py:517
  180.8 35.7 %weight_scatter.1 = f32[16,2048]{1,0:T(8,128)} custom-call(bf16[4,4,4,16,2048]{4,3,2,1,0:T(8,128)(2,1)} %bitcast.31), custom_call_target="tpu_custom_call" | custom-call | flops 1000000 | bytes 8000000 | tf_op jit(solution)/shard_map/weight_scatter/pallas_call | solution.py:211
  216.5 1.6 copy.40
  (3 shorter events, 0.1 us)
Async XLA Ops:
  2.4 17.0 %copy-start.1 = (bf16[128,2048]{1,0:T(8,128)(2,1)}, bf16[128,2048]{1,0:T(8,128)(2,1)S(1)}, u32[]{:S(2)}) copy-start(bf16[128,2048]{1,0:T(8,128)(2,1)S(1)} %broadcast_multiply_fusion.keep) | copy-start | bytes 1572868
  2.5 79.1 %collective-permute-start.1 = (bf16[128,2048]{1,0:T(8,128)(2,1)S(1)}, bf16[128,2048]{1,0:T(8,128)(2,1)S(1)}, u32[]{:S(2)}, u32[]{:S(2)}) collective-permute-start(bf16[128,2048]{1,0:T(8,128)(2,1)S(1)} %broadcast_multiply_fusion.keep), channel_id=1, source_target_pairs={{0,31},{1,30},{2,29},{3,28},{4,27},{5,26},{6,25},{7,24},{8,23},{9,... | collective-permute-start | bytes 1572872 | tf_op jit(solution)/shard_map/ppermute | solution.py:506
  66.2 108.8 %collective-permute-start.3 = (bf16[256,2048]{1,0:T(8,128)(2,1)}, bf16[256,2048]{1,0:T(8,128)(2,1)}, u32[]{:S(2)}, u32[]{:S(2)}) collective-permute-start(bf16[256,2048]{1,0:T(8,128)(2,1)} %bitcast.42), channel_id=1, source_target_pairs={{0,32},{32,0},{64,96},{96,64},{1,33},{33,1},{65,97},{97,65},{2,34}... | collective-permute-start | bytes 3145736 | tf_op jit(solution)/shard_map/ppermute | solution.py:516
  73.5 98.3 %collective-permute-start = (bf16[128,2048]{1,0:T(8,128)(2,1)}, bf16[128,2048]{1,0:T(8,128)(2,1)}, u32[]{:S(2)}, u32[]{:S(2)}) collective-permute-start(bf16[128,2048]{1,0:T(8,128)(2,1)} %get-tuple-element.72), channel_id=1, source_target_pairs={{0,31},{1,30},{2,29},{3,28},{4,27},{5,26},{6,25},{7,24},{8,23},{9,... | collective-permute-start | bytes 1572872 | tf_op jit(solution)/shard_map/ppermute | solution.py:506
  81.5 0.8 copy-start.2
  85.0 7.1 %copy-start = (bf16[2,128,2048]{2,1,0:T(8,128)(2,1)S(1)}, bf16[2,128,2048]{2,1,0:T(8,128)(2,1)}, u32[]{:S(2)}) copy-start(bf16[2,128,2048]{2,1,0:T(8,128)(2,1)} %flip_keep.1) | copy-start | bytes 3145732
  96.1 78.9 %collective-permute-start.2 = (bf16[256,1024]{0,1:T(8,128)(2,1)S(1)}, bf16[256,1024]{0,1:T(8,128)(2,1)S(1)}, u32[]{:S(2)}, u32[]{:S(2)}) collective-permute-start(bf16[256,1024]{0,1:T(8,128)(2,1)S(1)} %bitcast.32), channel_id=1, source_target_pairs={{0,32},{32,0},{64,96},{96,64},{1,33},{33,1},{65,97},{97,65},{2,34}... | collective-permute-start | bytes 1572872 | tf_op jit(solution)/shard_map/ppermute | solution.py:515
  142.8 6.4 %copy-start.4 = (f32[2,2,2048]{2,1,0:T(2,128)S(1)}, f32[2,2,2048]{2,1,0:T(2,128)}, u32[]{:S(2)}) copy-start(f32[2,2,2048]{2,1,0:T(2,128)} %get-tuple-element.50) | copy-start | bytes 98308
  167.9 6.4 %copy-start.3 = (f32[24,128]{1,0:T(8,128)S(1)}, f32[24,128]{1,0:T(8,128)}, u32[]{:S(2)}) copy-start(f32[24,128]{1,0:T(8,128)} %small_sum.1) | copy-start | bytes 36868
where the time goes:
time: 220 us; the launch traced here: 218 us
  Pallas kernels  162 us (74%)
  matrix products  19 us (9%)
  local copies, waits for them, and re-layouts  18.8 us (9%)
  starting transfers between devices  15.1 us (7%)
  other arithmetic  2.63 us (1%)
    pallas_call x1, Pallas kernels, state_scan(): pl.pallas_call(functools.partial(scan_kernel, False), out_shape=(bf, dec)...  39.7 us
    pallas_call x1, Pallas kernels, state_scan(): pl.pallas_call(kernel, out_shape=bf, in_specs=[vmem, vmem], out_specs=vme...  37 us
    pallas_call x1, Pallas kernels, weight_scatter(): pl.pallas_call(scatter_kernel, out_shape=jax.ShapeDtypeStruct((16, 2048),...  35.7 us
    pallas_call x1, Pallas kernels, small_sum(): pl.pallas_call(sum_kernel, out_shape=jax.ShapeDtypeStruct(shape, jnp.floa...  17.8 us
    ppermute x2, starting transfers between devices, mirror(): lax.ppermute(value, 'ctx', [(i, N_CTX - 1 - i) for i in range(N_CTX)])  14.5 us
    pallas_call x1, Pallas kernels, body(): strand_call(backward_kernel, 'backward', [proj, wide, wide, tok, spread_s...  9.23 us
    unnamed x15, local copies, waits for them, and re-layouts  7.19 us
    dot_general x1, matrix products, body(): jnp.einsum('srd,dk->srk', d_out, w_out, preferred_element_type=f32)  7.12 us
  transfers between devices with their start and end apart: 4, of which 0 were waited for; matrix products, arithmetic and copies ran while one was open for 14% of the time, Pallas kernels for 58%

commit v1 on v0

v1 whole, which is shorter than its diff:
```python
import functools

import jax
import jax.numpy as jnp
from jax import lax
from jax.experimental import pallas as pl
from jax.experimental.pallas import tpu as pltpu
from jax.sharding import PartitionSpec as P

MESH = pl.DeviceIdType.MESH
N_CTX = 32


CUTS = ((0, 768), (768, 1408), (1408, 2048))


def place():
    dp, ctx = lax.axis_index("dp"), lax.axis_index("ctx")
    x_lo, core = dp // 2, lax.rem(dp, 2)
    x_hi, z, y = ctx // 16, lax.rem(ctx // 4, 4), lax.rem(ctx, 4)
    return dp, core, {"x": x_lo * 2 + x_hi, "z": z, "y": y}


def line_peer(axis, k):
    dp, core, at = place()
    there = lax.rem(at[axis] + k, 4)
    x = there if axis == "x" else at["x"]
    z = there if axis == "z" else at["z"]
    y = there if axis == "y" else at["y"]
    return there, ((x // 2) * 2 + core, lax.rem(x, 2) * 16 + z * 4 + y)


def scatter_steps(s_ref, out_ref, scratch):
    (ra0, ra1, ra2, sa0, sa1, sa2, rb0, rb1, rb2, sb0, sb1, sb2, rc0, rc1, rc2, send_sem, recv_sem) = scratch
    _, _, at = place()
    cols = [pl.ds(a, b - a) for a, b in CUTS]
    axes = (("y", "z", "x"), ("z", "x", "y"), ("x", "y", "z"))

    def send(stage, part, k, pick, dst):
        there, device = line_peer(axes[part][stage], k)
        index = (stage * 3 + part) * 3 + k - 1
        copy = pltpu.make_async_remote_copy(
            src_ref=pick(there), dst_ref=dst.at[k - 1],
            send_sem=send_sem.at[index], recv_sem=recv_sem.at[index],
            device_id=device, device_id_type=MESH)
        copy.start()
        return copy

    def add(mine, recv, i):
        total = mine.astype(jnp.float32)
        for k in range(3):
            total = total + recv[(k,) + i].astype(jnp.float32)
        return total

    pending = {}

    def begin():
        picks = (
            lambda t: s_ref.at[:, :, t, :, cols[0]],
            lambda t: s_ref.at[:, t, :, :, cols[1]],
            lambda t: s_ref.at[t, :, :, :, cols[2]],
        )
        pending[0] = [[send(0, p, k, picks[p], (ra0, ra1, ra2)[p]) for k in (2, 1, 3)] for p in range(3)]

    def second():
        pending[1] = []
        for p in range(3):
            for copy in pending[0][p]:
                copy.wait()
            ra, sa = (ra0, ra1, ra2)[p], (sa0, sa1, sa2)[p]

            def step(i, c, p=p, ra=ra, sa=sa):
                a, b = i // 4, lax.rem(i, 4)
                if p == 0:
                    mine = s_ref[a, b, at["y"], :, cols[0]]
                elif p == 1:
                    mine = s_ref[a, at["z"], b, :, cols[1]]
                else:
                    mine = s_ref[at["x"], a, b, :, cols[2]]
                sa[a, b] = add(mine, ra, (a, b)).astype(jnp.bfloat16)
                return c

            lax.fori_loop(0, 16, step, 0)
            pick = (lambda t: sa0.at[:, t], lambda t: sa1.at[t], lambda t: sa2.at[:, t])[p]
            pending[1].append([send(1, p, k, pick, (rb0, rb1, rb2)[p]) for k in (2, 1, 3)])

    def third():
        pending[2] = []
        for p in range(3):
            for copy in pending[1][p]:
                copy.wait()
            rb, sb = (rb0, rb1, rb2)[p], (sb0, sb1, sb2)[p]
            for i in range(4):
                mine = (lambda: sa0[i, at["z"]], lambda: sa1[at["x"], i], lambda: sa2[i, at["y"]])[p]()
                sb[i] = add(mine, rb, (i,)).astype(jnp.bfloat16)
            pending[2].append([send(2, p, k, lambda t, sb=sb: sb.at[t], (rc0, rc1, rc2)[p]) for k in (2, 1, 3)])

    def end():
        for p in range(3):
            for copy in pending[2][p]:
                copy.wait()
            sb, rc = (sb0, sb1, sb2)[p], (rc0, rc1, rc2)[p]
            out_ref[:, cols[p]] = add(sb[at[axes[p][2]]], rc, ())

    return begin, second, third, end


def scan_steps(backward, s_ref, dec_ref, out_ref, got_dec, scratch):
    got, pre, send_a, recv_a, send_d, recv_d, send_b, recv_b, own_sem = scratch
    me = lax.axis_index("ctx")

    def peer_of(k):
        return lax.rem(me + k, N_CTX)

    def state_copy(src, dst, send, recv, strand_at):
        rows = pl.ds(P_SIZE * strand_at, P_SIZE)

        def make(k):
            return pltpu.make_async_remote_copy(
                src_ref=src.at[peer_of(k), rows], dst_ref=dst.at[me, rows],
                send_sem=send.at[strand_at, k], recv_sem=recv.at[strand_at, k],
                device_id={"ctx": peer_of(k)}, device_id_type=MESH)
        return make

    def copy_d(k):
        return pltpu.make_async_remote_copy(
            src_ref=dec_ref.at[peer_of(k)], dst_ref=got_dec.at[me], send_sem=send_d.at[k], recv_sem=recv_d.at[k],
            device_id={"ctx": peer_of(k)}, device_id_type=MESH)

    copy_a = [state_copy(s_ref, got, send_a, recv_a, i) for i in range(2)]
    copy_b = [state_copy(pre, out_ref, send_b, recv_b, i) for i in range(2)]

    def start(make):
        def step(k, c):
            make(k).start()
            return c
        lax.fori_loop(1, N_CTX, step, 0)

    def finish(make):
        def step(k, c):
            make(k).wait()
            return c
        lax.fori_loop(1, N_CTX, step, 0)

    def begin():
        if not backward:
            start(copy_d)
        for i in range(2):
            start(copy_a[i])
        own = pltpu.make_async_copy(s_ref.at[me], got.at[me], own_sem.at[0])
        own.start()
        own.wait()
        if not backward:
            own_d = pltpu.make_async_copy(dec_ref.at[me], got_dec.at[me], own_sem.at[1])
            own_d.start()
            own_d.wait()

    def turn():
        if not backward:
            finish(copy_d)
        decays = dec_ref if backward else got_dec
        for i in range(2):
            finish(copy_a[i])
            rows = slice(P_SIZE * i, P_SIZE * i + P_SIZE)

            def fold(n, carry, i=i, rows=rows):
                at = N_CTX - 1 - n if backward else n
                pre[at, rows, :] = carry.astype(jnp.bfloat16)
                return decays[at, 8 * i : 8 * i + 1, :] * carry + got[at, rows, :].astype(jnp.float32)

            lax.fori_loop(0, N_CTX, fold, jnp.zeros((P_SIZE, NS), jnp.float32))
            start(copy_b[i])

    def end():
        own = pltpu.make_async_copy(pre.at[me], out_ref.at[me], own_sem.at[2])
        own.start()
        own.wait()
        for i in range(2):
            finish(copy_b[i])

    return begin, turn, end


def greet_line():
    me = lax.axis_index("ctx")
    barrier = pltpu.get_barrier_semaphore()

    def step(k, c):
        pl.semaphore_signal(barrier, inc=1, device_id={"ctx": lax.rem(me + k, N_CTX)}, device_id_type=MESH)
        return c

    lax.fori_loop(1, N_CTX, step, 0)
    pl.semaphore_wait(barrier, N_CTX - 1)


def forward_exchange(s_ref, dec_ref, out_ref, got_dec, *scratch):
    begin, turn, end = scan_steps(False, s_ref, dec_ref, out_ref, got_dec, scratch)
    greet_line()
    begin()
    turn()
    end()


def backward_exchange(s_ref, dec_ref, grads, grads_other, normed, normed_other, out_ref, partial, *scratch):
    begin, turn, end = scan_steps(True, s_ref, dec_ref, out_ref, None, scratch)
    greet_line()
    begin()

    def rows(i, c):
        at = pl.ds(pl.multiple_of(i * 256, 128), 256)
        total = dot(grads[:, at], normed[...], ROWS) + dot(grads_other[:, at], normed_other[...], ROWS)
        partial[i] = total.astype(jnp.bfloat16).reshape(4, 4, 16, 2048)
        return c

    lax.fori_loop(0, 4, rows, 0)
    turn()
    end()


def last_exchange(v_ref, weight, out_v, d_weight, plane, line, part, send_a, recv_a, send_b, recv_b, *scratch):
    w_begin, w_second, w_third, w_end = scatter_steps(weight, d_weight, scratch)
    dp, ctx = lax.axis_index("dp"), lax.axis_index("ctx")
    q, x_hi = lax.rem(ctx, 16), ctx // 16
    e = x_hi * 4 + dp

    def peer_a(k):
        return (dp, x_hi * 16 + lax.rem(q + k, 16))

    def peer_b(k):
        there = lax.rem(e + k, 8)
        return (lax.rem(there, 4), (there // 4) * 16 + q)

    barrier = pltpu.get_barrier_semaphore()
    peers = [peer_a(k) for k in range(1, 16)] + [peer_b(k) for k in range(1, 8)]
    peers += [line_peer(axis, k)[1] for axis in "xyz" for k in (1, 2, 3)]
    for device in peers:
        pl.semaphore_signal(barrier, inc=1, device_id=device, device_id_type=MESH)
    pl.semaphore_wait(barrier, len(peers))

    def copy_a(k):
        return pltpu.make_async_remote_copy(
            src_ref=v_ref, dst_ref=plane.at[q], send_sem=send_a.at[k], recv_sem=recv_a.at[k],
            device_id=peer_a(k), device_id_type=MESH)

    def copy_b(k):
        return pltpu.make_async_remote_copy(
            src_ref=part, dst_ref=line.at[e], send_sem=send_b.at[k], recv_sem=recv_b.at[k],
            device_id=peer_b(k), device_id_type=MESH)

    first = [copy_a(k) for k in range(1, 16)]
    for copy in first:
        copy.start()
    w_begin()
    plane[q] = v_ref[...]
    for copy in first:
        copy.wait()
    total = plane[0]
    for i in range(1, 16):
        total = total + plane[i]
    part[...] = total
    line[e] = total
    second = [copy_b(k) for k in range(1, 8)]
    for copy in second:
        copy.start()
    w_second()
    for copy in second:
        copy.wait()
    total = line[0]
    for i in range(1, 8):
        total = total + line[i]
    out_v[...] = total
    w_third()
    w_end()


def exchange_call(kernel, name, collective_id, out_shape, scratch, *args):
    vmem = pl.BlockSpec(memory_space=pltpu.VMEM)
    return pl.pallas_call(
        kernel, out_shape=out_shape, in_specs=[vmem] * len(args), out_specs=[vmem] * len(out_shape),
        scratch_shapes=scratch, name=name,
        compiler_params=pltpu.CompilerParams(collective_id=collective_id, has_side_effects=True),
        cost_estimate=pl.CostEstimate(flops=1000000, bytes_accessed=4000000, transcendentals=0))(*args)


def scan_scratch():
    dma = pltpu.SemaphoreType.DMA
    state = pltpu.VMEM((N_CTX, 128, 128), jnp.bfloat16)
    pairs, singles = dma((2, N_CTX)), dma((N_CTX,))
    return [state, state, pairs, pairs, singles, singles, pairs, pairs, dma((3,))]


def sum_scratch(shape):
    dma = pltpu.SemaphoreType.DMA
    return [
        pltpu.VMEM((16,) + shape, jnp.float32), pltpu.VMEM((8,) + shape, jnp.float32),
        pltpu.VMEM(shape, jnp.float32), dma((16,)), dma((16,)), dma((8,)), dma((8,))]


def scatter_scratch():
    widths = [b - a for a, b in CUTS]
    shapes = ((3, 4, 4, 16), (4, 4, 16), (3, 4, 16), (4, 16), (3, 16))
    scratch = [pltpu.VMEM(shape + (w,), jnp.bfloat16) for shape in shapes for w in widths]
    return scratch + [pltpu.SemaphoreType.DMA((27,)), pltpu.SemaphoreType.DMA((27,))]


H = 32
P_SIZE = 64
NS = 128
DI = 2048
Q = 128
PAIRS = 16
B_AT = 2 * DI
C_AT = 2 * DI + NS
bf16 = jnp.bfloat16
f32 = jnp.float32
precise = lax.Precision.HIGHEST


def dot(a, b, dims=((1,), (0,)), precision=None):
    return lax.dot_general(a, b, (dims, ((), ())), precision=precision, preferred_element_type=f32)


ROWS = ((0,), (0,))
LANES = ((1,), (1,))


def iota(shape, axis):
    return lax.broadcasted_iota(jnp.int32, shape, axis)


def head_map():
    return (iota((H, DI), 0) == iota((H, DI), 1) // P_SIZE).astype(f32).astype(bf16)


def expand(value, heads):
    high = value.astype(bf16)
    low = (value - high.astype(f32)).astype(bf16)
    return dot(high, heads) + dot(low, heads)


def per_head(value, heads):
    return dot(value.astype(bf16), heads, LANES)


def softplus(value):
    return jnp.maximum(value, 0.0) + jnp.log1p(jnp.exp(-jnp.abs(value)))


def sigmoid(value):
    return 1.0 / (1.0 + jnp.exp(-value))


def tril():
    return iota((Q, Q), 0) >= iota((Q, Q), 1)


def half_masks():
    left = (iota((Q, 128), 1) < P_SIZE).astype(f32)
    return left.astype(bf16), (1.0 - left).astype(bf16)


def summary_kernel(proj, dt_raw, a_log, bias, state, decay, dt_out, run_out, dt_t_out, run_t_out):
    lower = tril().astype(f32)
    same = (iota((Q, Q), 0) == iota((Q, Q), 1)).astype(f32)
    dt = softplus(dt_raw[0].astype(f32) + bias[...])
    run = dot(lower, -jnp.exp(a_log[...]) * dt, precision=precise)
    run_t = dot(run, same, ROWS, precision=precise)
    dt_out[0] = dt
    run_out[0] = run
    dt_t_out[0] = dot(dt, same, ROWS, precision=precise)
    run_t_out[0] = run_t
    weight = jnp.exp(run[Q - 1 : Q, :] - run) * dt
    weighed = (expand(weight, head_map()) * proj[0, :, DI:B_AT].astype(f32)).astype(bf16)
    total = dot(weighed, proj[0, :, B_AT:C_AT], ROWS)
    state[...] = total.astype(bf16).reshape(H, P_SIZE, NS)
    left = jnp.exp(run_t[:, Q - 1 : Q])
    for h in range(H):
        decay[h] = jnp.broadcast_to(left[h : h + 1, :], (8, 128))


def forward_kernel(proj, run, dt_t, run_t, entering, skip, gain, normed, y_out, spread_out, mix_out, local):
    write, read = proj[0, :, B_AT:C_AT], proj[0, :, C_AT:]
    affinity = dot(read, write, LANES)
    affinity = jnp.concatenate([affinity, affinity], 1)
    causal = tril()
    left, right = half_masks()
    for j in range(PAIRS):
        cols = slice(DI + 128 * j, DI + 128 * j + 128)
        both = []
        for h in (2 * j, 2 * j + 1):
            gap = run[0, :, h : h + 1] - run_t[0, h : h + 1, :]
            both.append(jnp.exp(jnp.where(causal, gap, -1e30)) * dt_t[0, h : h + 1, :])
        spread = jnp.concatenate(both, 1)
        spread_out[0, j] = spread.astype(bf16)
        values = proj[0, :, cols]
        stacked = jnp.concatenate([values * left, values * right], 0)
        mixing = (spread * affinity).astype(bf16)
        mix_out[0, j] = mixing
        local[:, 128 * j : 128 * j + 128] = dot(mixing, stacked)
    carried = dot(read, entering[...].reshape(DI, NS), LANES)
    grown = expand(jnp.exp(run[0]), head_map())
    y = local[...] + grown * carried + skip[...] * proj[0, :, DI:B_AT].astype(f32)
    y_out[0] = y
    gate = proj[0, :, :DI].astype(f32)
    gated = y * gate * sigmoid(gate)
    inv = lax.rsqrt(jnp.mean(gated * gated, axis=1, keepdims=True) + 1e-05)
    normed[0] = (gated * inv * gain[...]).astype(bf16)


def backward_kernel(proj, y_in, d_normed, run, spread_in, mix_in, entering, skip, gain,
                    d_gate, d_x, d_entering, d_write, d_read, gains, from_y, from_x, dy_keep, dx_keep):
    heads = head_map()
    gate = proj[0, :, :DI].astype(f32)
    y = y_in[0]
    sig = sigmoid(gate)
    silu = gate * sig
    gated = y * silu
    inv = lax.rsqrt(jnp.mean(gated * gated, axis=1, keepdims=True) + 1e-05)
    dn = d_normed[0].astype(f32)
    gains[0, 0:1, :] = jnp.sum(dn * (gated * inv), axis=0, keepdims=True)
    up = dn * gain[...]
    pull = jnp.mean(up * gated, axis=1, keepdims=True) * (inv * inv * inv)
    d_gated = inv * up - gated * pull
    dy = d_gated * silu
    d_gate[0] = (d_gated * y * (sig * (1.0 + gate * (1.0 - sig)))).astype(bf16)
    values = proj[0, :, DI:B_AT].astype(f32)
    gains[0, 1:2, :] = jnp.sum(dy * values, axis=0, keepdims=True)
    dy_keep[...] = dy.astype(bf16)
    from_y[0] = per_head(dy_keep[...].astype(f32) * (y - skip[...] * values), heads)
    grown = (expand(jnp.exp(run[0]), heads) * dy).astype(bf16)
    write, read = proj[0, :, B_AT:C_AT], proj[0, :, C_AT:]
    state = entering[...].reshape(DI, NS)
    d_entering[...] = dot(grown, read, ROWS).astype(bf16).reshape(H, P_SIZE, NS)
    d_c = dot(grown, state)
    left, right = half_masks()
    first = iota((Q, 128), 1) < P_SIZE
    d_aff = jnp.zeros((Q, Q), f32)
    for j in range(PAIRS):
        cols = slice(128 * j, 128 * j + 128)
        dyp = dy_keep[:, cols]
        x = proj[0, :, DI + 128 * j : DI + 128 * j + 128]
        stacked = jnp.concatenate([x * left, x * right], 0)
        d_mix = dot(dyp, stacked, LANES) * spread_in[0, j].astype(f32)
        d_aff = d_aff + d_mix[:, :Q] + d_mix[:, Q:]
        back = dot(mix_in[0, j], dyp, ROWS)
        dx_keep[:, cols] = jnp.where(first, back[:Q], back[Q:])
    d_aff = d_aff.astype(bf16)
    d_read[0] = (d_c + dot(d_aff, write)).astype(bf16)
    d_write[0] = dot(d_aff, read, ROWS)
    dx = dx_keep[...]
    from_x[0] = per_head(values * dx, heads)
    d_x[0] = dx + skip[...] * dy


def finish_kernel(proj, dt_raw, dt_in, run_in, leaving, entering, from_y, from_x, d_x, d_gate, d_write, d_read,
                  a_log, bias, d_proj, d_dt, sums):
    heads = head_map()
    rate = jnp.exp(a_log[...])
    dt, run = dt_in[0], run_in[0]
    last = run[Q - 1 : Q, :]
    weight = expand(jnp.exp(last - run) * dt, heads)
    values = proj[0, :, DI:B_AT].astype(f32)
    out = leaving[...].reshape(DI, NS)
    d_state = weight * dot(proj[0, :, B_AT:C_AT], out, LANES)
    d_b = d_write[0] + dot((weight * values).astype(bf16), out)
    d_proj[0, :, :DI] = d_gate[0]
    d_proj[0, :, DI:B_AT] = (d_x[0] + d_state).astype(bf16)
    d_proj[0, :, B_AT:C_AT] = d_b.astype(bf16)
    d_proj[0, :, C_AT:] = d_read[0]
    from_state = per_head(values * d_state, heads)
    total = from_x[0] + from_state
    meet = jnp.sum(entering[...].astype(f32) * leaving[...].astype(f32), axis=1)
    meet = dot(jnp.ones((8, NS), f32), meet, LANES, precision=precise)[0:1, :]
    d_last = jnp.exp(last) * meet + jnp.sum(from_state, axis=0, keepdims=True)
    upper = (iota((Q, Q), 0) <= iota((Q, Q), 1)).astype(f32)
    d_log = dot(upper, from_y[0] - total, precision=precise) + d_last
    d_step = total / dt - rate * d_log
    d_raw = d_step * sigmoid(dt_raw[0].astype(f32) + bias[...])
    d_dt[0] = d_raw.astype(bf16)
    sums[0, 0:1, :] = jnp.sum(d_log * (-rate * dt), axis=0, keepdims=True)
    sums[0, 1:2, :] = jnp.sum(d_raw, axis=0, keepdims=True)


def strand(*shape):
    return pl.BlockSpec((1,) + shape, lambda s: (s,) + (0,) * len(shape))


def shared(*shape):
    return pl.BlockSpec(shape, lambda s: (0,) * len(shape))


STATE = pl.BlockSpec((H, P_SIZE, NS), lambda s: (0, s, 0))


def like(dtype, *shape):
    return jax.ShapeDtypeStruct(shape, dtype)


def strand_call(kernel, name, in_specs, out_specs, out_shape, scratch=(), flops=2000000000):
    return pl.pallas_call(
        kernel, grid=(2,), in_specs=in_specs, out_specs=out_specs, out_shape=out_shape,
        scratch_shapes=list(scratch), name=name,
        cost_estimate=pl.CostEstimate(flops=flops, bytes_accessed=10000000, transcendentals=0))


def flipped(block):
    turn = (iota((128, 128), 0) + iota((128, 128), 1) == 127).astype(f32).astype(bf16)
    rows = dot(turn, block).astype(bf16)
    parts = [dot(rows[:, 128 * j : 128 * j + 128], turn) for j in range(15, -1, -1)]
    return jnp.concatenate(parts, 1)


def flip_kernel(keep, got, out, mine, theirs):
    out[0] = keep[...]
    out[1] = flipped(got[...]).astype(bf16)
    core = lax.rem(lax.axis_index("dp"), 2)
    for s in range(2):
        for half in range(2):
            rows, cols = slice(Q * s, Q * s + Q), slice(512 * half, 512 * half + 512)
            mine[rows, cols] = out[s, :, pl.ds(pl.multiple_of((2 * half + core) * 512, 128), 512)]
            theirs[rows, cols] = out[s, :, pl.ds(pl.multiple_of((2 * half + 1 - core) * 512, 128), 512)]


def mix_kernel(own, got, out):
    out[...] = (own[...].astype(f32) + flipped(got[...])).astype(bf16)


def whole_call(kernel, name, out_shape, *args):
    vmem = pl.BlockSpec(memory_space=pltpu.VMEM)
    return pl.pallas_call(
        kernel, out_shape=out_shape, in_specs=[vmem] * len(args), out_specs=jax.tree.map(lambda _: vmem, out_shape), name=name,
        cost_estimate=pl.CostEstimate(flops=200000000, bytes_accessed=2000000, transcendentals=0))(*args)


def mirror(value):
    return lax.ppermute(value, "ctx", [(i, N_CTX - 1 - i) for i in range(N_CTX)])


def other_core(value):
    return lax.ppermute(value, "dp", [(i, i ^ 1) for i in range(4)])


def body(projections, dt_raw, a_log, dt_bias, skip_gain, norm_gain, w_out, base_ids, cotangent):
    keep = cotangent * (base_ids != 4).astype(bf16)[:, None]
    got_keep = mirror(keep)
    proj, tok = strand(Q, 2 * DI + 2 * NS), strand(Q, H)
    tok_t, wide = strand(H, Q), strand(Q, DI)
    row, lane = shared(1, H), shared(1, DI)
    skip, gain = jnp.repeat(skip_gain, P_SIZE)[None], norm_gain[None]
    state, factor, dt, run, dt_t, run_t = strand_call(
        summary_kernel, "summary", [proj, tok, row, row],
        [STATE, pl.BlockSpec((H, 8, NS), lambda s: (0, s, 0)), tok, tok, tok_t, tok_t],
        [like(bf16, H, 2 * P_SIZE, NS), like(f32, H, 16, NS), like(f32, 2, Q, H), like(f32, 2, Q, H),
         like(f32, 2, H, Q), like(f32, 2, H, Q)],
    )(projections, dt_raw, a_log[None], dt_bias[None])
    states = like(bf16, H, 2 * P_SIZE, NS)
    entering, decays = exchange_call(
        forward_exchange, "forward_exchange", 1, [states, like(f32, H, 16, NS)], scan_scratch(), state, factor)
    d_out, grads, grads_away = whole_call(
        flip_kernel, "flip_keep", [like(bf16, 2, Q, DI)] + [like(bf16, 2 * Q, DI // 2)] * 2, keep, got_keep)
    spread_spec = strand(PAIRS, Q, 2 * Q)
    normed, y, spread, mixing = strand_call(
        forward_kernel, "forward", [proj, tok, tok_t, tok_t, STATE, lane, lane],
        [wide, wide, spread_spec, spread_spec],
        [like(bf16, 2, Q, DI), like(f32, 2, Q, DI), like(bf16, 2, PAIRS, Q, 2 * Q),
         like(bf16, 2, PAIRS, Q, 2 * Q)],
        [pltpu.VMEM((Q, DI), f32)],
    )(projections, run, dt_t, run_t, entering, skip, gain)
    strand_out = jnp.einsum("srk,dk->srd", normed, w_out, preferred_element_type=f32).astype(bf16)
    moved = mirror(strand_out[1])
    d_normed = jnp.einsum("srd,dk->srk", d_out, w_out, preferred_element_type=f32).astype(bf16)
    d_gate, d_x, d_entering, d_write, d_read, gains, from_y, from_x = strand_call(
        backward_kernel, "backward", [proj, wide, wide, tok, spread_spec, spread_spec, STATE, lane, lane],
        [wide, wide, STATE, strand(Q, NS), strand(Q, NS), strand(2, DI), tok, tok],
        [like(bf16, 2, Q, DI), like(f32, 2, Q, DI), like(bf16, H, 2 * P_SIZE, NS), like(f32, 2, Q, NS),
         like(bf16, 2, Q, NS), like(f32, 2, 2, DI), like(f32, 2, Q, H), like(f32, 2, Q, H)],
        [pltpu.VMEM((Q, DI), bf16), pltpu.VMEM((Q, DI), f32)],
    )(projections, y, d_normed, run, spread, mixing, entering, skip, gain)
    flat = normed.reshape(2 * Q, DI)
    leaving, partial = exchange_call(
        backward_exchange, "backward_exchange", 2, [states, like(bf16, 4, 4, 4, 16, DI)], scan_scratch(),
        d_entering, decays, grads, other_core(grads_away), flat, other_core(flat))
    mixed_out = whole_call(mix_kernel, "mix", like(bf16, Q, DI), strand_out[0], moved)
    d_proj, d_dt, sums = strand_call(
        finish_kernel, "finish",
        [proj, tok, tok, tok, STATE, STATE, tok, tok, wide, wide, strand(Q, NS), strand(Q, NS), row, row],
        [proj, tok, strand(2, H)],
        [like(bf16, 2, Q, 2 * DI + 2 * NS), like(bf16, 2, Q, H), like(f32, 2, 2, H)],
    )(projections, dt_raw, dt, run, leaving, entering, from_y, from_x, d_x, d_gate, d_write, d_read,
      a_log[None], dt_bias[None])
    gains = jnp.sum(gains, axis=0)
    d_skip = jnp.sum(gains[1].reshape(H, P_SIZE), axis=1)
    small = jnp.concatenate([gains[0], jnp.sum(sums, axis=0).reshape(-1), d_skip, jnp.zeros((928,), f32)])
    summed, d_w_out = exchange_call(
        last_exchange, "last_exchange", 3, [like(f32, 24, 128), like(f32, 16, DI)],
        sum_scratch((24, 128)) + scatter_scratch(), small.reshape(24, 128), partial)
    summed = summed.reshape(-1)
    return (mixed_out, d_proj, d_dt, d_w_out, summed[2048 : 2048 + 96].reshape(3, 32), summed[:2048])


def solution(mesh):
    placed = (
        P(None, ("dp", "ctx"), None),
        P(None, ("dp", "ctx"), None),
        P(),
        P(),
        P(),
        P(),
        P(),
        P(("dp", "ctx")),
        P(("dp", "ctx"), None),
    )
    return jax.shard_map(
        body,
        mesh=mesh,
        in_specs=placed,
        out_specs=(
            P(("dp", "ctx"), None),
            P(None, ("dp", "ctx"), None),
            P(None, ("dp", "ctx"), None),
            P(("dp", "ctx"), None),
            P(),
            P(),
        ),
        check_vma=False,
    )
```

time: 220 us -> 199 us (0.905)
  Pallas kernels: 162 us -> 152 us
  local copies, waits for them, and re-layouts: 18.8 us -> 12.3 us
  matrix products: 19 us -> 13.1 us
    pallas_call x6 -> x5, Pallas kernels: 142 us -> 131 us  [the longest x3 119 us: exchange_call(): pl.pallas_call(kernel, out_shape=out_shape, in_specs=[vmem] * len(args),...]
    dot_general x1 -> x0, matrix products: 5.83 us -> none  [weight_grad(): lax.dot_general(grads_two, normed_two, (((0,), (0,)), ((), ())), preferre...]
    broadcast_in_dim x3 -> x0, local copies, waits for them, and re-layouts: 3.28 us -> none  [the longest x2 1.95 us: body(): rate[:, None]]
  transfers between devices with their start and end apart: 4 -> 4, of which waited for: 0 -> 0; matrix products, arithmetic and copies ran while one was open for 14% -> 9% of each run, Pallas kernels for 58% -> 34%
where the time goes in v1:
time: 199 us; the launch traced here: 197 us
  Pallas kernels  152 us (76%)
  starting transfers between devices  15.6 us (8%)
  matrix products  13.1 us (7%)
  local copies, waits for them, and re-layouts  12.3 us (6%)
  other arithmetic  3.43 us (2%)
    pallas_call x3, Pallas kernels, exchange_call(): pl.pallas_call(kernel, out_shape=out_shape, in_specs=[vmem] * len(args),...  119 us
    ppermute x2, starting transfers between devices, mirror(): lax.ppermute(value, 'ctx', [(i, N_CTX - 1 - i) for i in range(N_CTX)])  15.3 us
    pallas_call x1, Pallas kernels, body(): strand_call(backward_kernel, 'backward', [proj, wide, wide, tok, spread_s...  9.17 us
    pallas_call x1, Pallas kernels, body(): strand_call(forward_kernel, 'forward', [proj, tok, tok_t, tok_t, STATE, l...  7.11 us
    dot_general x1, matrix products, body(): jnp.einsum('srd,dk->srk', d_out, w_out, preferred_element_type=f32)  7.03 us
    unnamed x15, local copies, waits for them, and re-layouts  6.45 us
    dot_general x1, matrix products, body(): jnp.einsum('srk,dk->srd', normed, w_out, preferred_element_type=f32)  6.08 us
    pallas_call x2, Pallas kernels, whole_call(): pl.pallas_call(kernel, out_shape=out_shape, in_specs=[vmem] * len(args),...  5.81 us
  transfers between devices with their start and end apart: 4, of which 0 were waited for; matrix products, arithmetic and copies ran while one was open for 9% of the time, Pallas kernels for 34%

profile of v1, /device:TPU:4, one launch (start us, length us, event | category | flops | bytes accessed | tf_op | source)
XLA Modules:
  0.0 196.7 jit_solution(14116256469675716141)
XLA Ops:
  0.6 0.7 compare_convert_fusion
  1.3 1.1 broadcast_multiply_fusion.keep
  2.4 0.0 copy-start
  2.5 6.5 %collective-permute-start.1 = (bf16[128,2048]{1,0:T(8,128)(2,1)S(1)}, bf16[128,2048]{1,0:T(8,128)(2,1)S(1)}, u32[]{:S(2)}, u32[]{:S(2)}) collective-permute-start(bf16[128,2048]{1,0:T(8,128)(2,1)S(1)} %broadcast_multiply_fusion.keep), channel_id=1, source_target_pairs={{0,31},{1,30},{2,29},{3,28},{4,27},{5,26},{6,25},{7,24},{8,23},{9,... | collective-permute-start | bytes 1572872 | tf_op jit(solution)/shard_map/ppermute | solution.py:536
  9.0 1.4 copy.21.dt_raw
  10.4 0.7 broadcast_in_dim.20
  11.1 0.7 broadcast_in_dim_reshape.3.skip
  11.8 4.5 %summary.1 = (bf16[32,128,128]{2,1,0:T(8,128)(2,1)}, f32[32,16,128]{2,1,0:T(8,128)}, f32[2,128,32]{2,1,0:T(8,128)}, f32[2,128,32]{2,1,0:T(8,128)}, f32[2,32,128]{2,1,0:T(8,128)}, /*index=5*/f32[2,32,128]{2,1,0:T(8,128)}) custom-call(bf16[2,128,4352]{2,1,0:T(8,128)(2,1)} %proj.7, bf16[2,128,32]{2,1,0:T(8,128)(2,1)} %copy.21.dt_raw, f32[1,32]{1,0:T(1,128)} %bitcast.29, ...), custom_call_target="tpu_custom_call" | custom-call | flops 2000000000 | bytes 10000000 | tf_op jit(solution)/shard_map/summary/pallas_call | solution.py:550
  16.3 40.8 %forward_exchange.1 = (bf16[32,128,128]{2,1,0:T(8,128)(2,1)}, f32[32,16,128]{2,1,0:T(8,128)}) custom-call(bf16[32,128,128]{2,1,0:T(8,128)(2,1)} %get-tuple-element.39.s_ref, f32[32,16,128]{2,1,0:T(8,128)} %get-tuple-element.40.dec_ref), custom_call_target="tpu_custom_call" | custom-call | flops 1000000 | bytes 4000000 | tf_op jit(solution)/shard_map/forward_exchange/pallas_call | solution.py:278
  57.1 0.0 copy-done
  57.1 7.1 %forward.1 = (bf16[2,128,2048]{2,1,0:T(8,128)(2,1)}, f32[2,128,2048]{2,1,0:T(8,128)}, bf16[2,16,128,256]{3,2,1,0:T(8,128)(2,1)}, bf16[2,16,128,256]{3,2,1,0:T(8,128)(2,1)}) custom-call(bf16[2,128,4352]{2,1,0:T(8,128)(2,1)} %proj.7, f32[2,128,32]{2,1,0:T(8,128)} %get-tuple-element.36.run.run_in, f32[2,32,128]{2,1,0:T(8,128)} %get-tuple-element.37.dt_t, ...), custom_call_target="tpu_custom_call" | custom-call | flops 2000000000 | bytes 10000000 | tf_op jit(solution)/shard_map/forward/pallas_call | solution.py:562
  64.2 0.1 collective-permute-start.3
  64.3 6.1 %fusion.4 = bf16[2,128,2048]{2,1,0:T(8,128)(2,1)S(1)} fusion(bf16[2,128,2048]{2,1,0:T(8,128)(2,1)} %get-tuple-element.42, bf16[2048,2048]{1,0:T(8,128)(2,1)} %param.15), kind=kOutput, calls=%fused_computation.4 | convolution fusion | flops 2148007936 | bytes 10485760 | tf_op jit(solution)/shard_map/srk,dk->srd/dot_general | solution.py:569
  70.4 0.9 slice_bitcast_fusion
  71.3 8.8 %collective-permute-start = (bf16[128,2048]{1,0:T(8,128)(2,1)S(1)}, bf16[128,2048]{1,0:T(8,128)(2,1)S(1)}, u32[]{:S(2)}, u32[]{:S(2)}) collective-permute-start(bf16[128,2048]{1,0:T(8,128)(2,1)S(1)} %get-tuple-element.84), channel_id=1, source_target_pairs={{0,31},{1,30},{2,29},{3,28},{4,27},{5,26},{6,25},{7,24},{8,23},{9,... | collective-permute-start | bytes 1572872 | tf_op jit(solution)/shard_map/ppermute | solution.py:536
  80.0 0.0 collective-permute-done.1.got
  80.0 0.0 copy-start.4
  80.0 0.8 copy-done.4
  80.9 3.3 %flip_keep.1 = (bf16[2,128,2048]{2,1,0:T(8,128)(2,1)}, bf16[256,1024]{1,0:T(8,128)(2,1)}, bf16[256,1024]{1,0:T(8,128)(2,1)}) custom-call(bf16[128,2048]{1,0:T(8,128)(2,1)} %copy-done, bf16[128,2048]{1,0:T(8,128)(2,1)} %copy-done.4), custom_call_target="tpu_custom_call" | custom-call | flops 200000000 | bytes 2000000 | tf_op jit(solution)/shard_map/flip_keep/pallas_call | solution.py:530
  84.1 0.2 collective-permute-start.2
  84.3 7.0 %fusion.7.d_normed = bf16[2,128,2048]{2,1,0:T(8,128)(2,1)} fusion(bf16[2,128,2048]{2,1,0:T(8,128)(2,1)} %get-tuple-element.45, bf16[2048,2048]{1,0:T(8,128)(2,1)} %param.15), kind=kOutput, calls=%fused_computation.5 | convolution fusion | flops 2148007936 | bytes 10485760 | tf_op jit(solution)/shard_map/srd,dk->srk/dot_general | solution.py:571
  91.4 9.2 %backward.1 = (bf16[2,128,2048]{2,1,0:T(8,128)(2,1)}, f32[2,128,2048]{2,1,0:T(8,128)}, bf16[32,128,128]{2,1,0:T(8,128)(2,1)}, f32[2,128,128]{2,1,0:T(8,128)}, bf...) custom-call(bf16[2,128,4352]{2,1,0:T(8,128)(2,1)} %proj.7, ...), custom_call_target="tpu_custom_call" | custom-call | flops 2000000000 | bytes 10000000 | tf_op jit(solution)/shard_map/backward/pallas_call | solution.py:572
  100.5 0.8 reduce_sum.27
  101.4 0.1 reshape_squeeze.3
  101.4 0.1 reduce_sum.29
  101.5 0.0 collective-permute-done.got
  101.6 0.0 copy-start.3
  101.6 0.8 copy-done.3
  102.3 2.6 %mix.1 = bf16[128,2048]{1,0:T(8,128)(2,1)} custom-call(bf16[128,2048]{1,0:T(8,128)(2,1)} %get-tuple-element.85.own, bf16[128,2048]{1,0:T(8,128)(2,1)} %copy-done.3), custom_call_target="tpu_custom_call" | custom-call | flops 200000000 | bytes 2000000 | tf_op jit(solution)/shard_map/mix/pallas_call | solution.py:530
  104.9 0.0 collective-permute-done.3.normed_other
  104.9 0.0 copy-start.1
  104.9 0.0 collective-permute-done.2.grads_other
  104.9 0.0 copy-start.2
  104.9 1.0 copy-done.1
  105.9 0.2 copy-done.2
  106.1 36.5 %backward_exchange.1 = (bf16[32,128,128]{2,1,0:T(8,128)(2,1)}, bf16[4,4,4,16,2048]{4,3,2,1,0:T(8,128)(2,1)}) custom-call(bf16[32,128,128]{2,1,0:T(8,128)(2,1)} %get-tuple-element.48.s_ref, f32[32,16,128]{2,1,0:T(8,128)} %get-tuple-element.49.dec_ref, bf16[256,1024]{1,0:T(8,128)(2,1)} %get-tuple-element.50.grads, bf16[256,1024]{1,0:T(8,128)(2,1)} %copy-done.2, ...), custom_call_target="tpu_custom_call" | custom-call | flops 1000000 | bytes 4000000 | tf_op jit(solution)/shard_map/backward_exchange/pallas_call | solution.py:278
  142.5 5.6 %finish.1 = (bf16[2,128,4352]{2,1,0:T(8,128)(2,1)}, bf16[2,128,32]{2,1,0:T(8,128)(2,1)}, f32[2,2,32]{2,1,0:T(2,128)}) custom-call(bf16[2,128,4352]{2,1,0:T(8,128)(2,1)} %proj.7, bf16[2,128,32]{2,1,0:T(8,128)(2,1)} %copy.21.dt_raw, f32[2,128,32]{2,1,0:T(8,128)} %get-tuple-element.43.dt_in, f32[2,128,32]{2,1,0:T(8,128)} %get-tuple-element.36.run.run_in, ...), custom_call_target="tpu_custom_call" | custom-call | flops 2000000000 | bytes 10000000 | tf_op jit(solution)/shard_map/finish/pallas_call | solution.py:584
  148.2 0.0 copy-start.5
  148.2 0.7 reduce_sum.28
  148.9 0.1 reshape.28
  149.0 0.7 concatenate.3
  149.7 42.1 %last_exchange.1 = (f32[24,128]{1,0:T(8,128)}, f32[16,2048]{1,0:T(8,128)}) custom-call(f32[24,128]{1,0:T(8,128)} %bitcast.25, bf16[4,4,4,16,2048]{4,3,2,1,0:T(8,128)(2,1)} %get-tuple-element.63.weight), custom_call_target="tpu_custom_call" | custom-call | flops 1000000 | bytes 4000000 | tf_op jit(solution)/shard_map/last_exchange/pallas_call | solution.py:278
  191.8 0.8 slice.28
  192.5 1.3 slice_bitcast_fusion.2
  193.8 0.6 slice.36
  194.4 0.0 copy-done.5
  194.4 0.7 copy.23
  195.1 1.6 copy.25
  (2 shorter events, 0.0 us)
Async XLA Ops:
  2.4 54.6 %copy-start = (bf16[128,2048]{1,0:T(8,128)(2,1)}, bf16[128,2048]{1,0:T(8,128)(2,1)S(1)}, u32[]{:S(2)}) copy-start(bf16[128,2048]{1,0:T(8,128)(2,1)S(1)} %broadcast_multiply_fusion.keep) | copy-start | bytes 1572868
  2.5 77.6 %collective-permute-start.1 = (bf16[128,2048]{1,0:T(8,128)(2,1)S(1)}, bf16[128,2048]{1,0:T(8,128)(2,1)S(1)}, u32[]{:S(2)}, u32[]{:S(2)}) collective-permute-start(bf16[128,2048]{1,0:T(8,128)(2,1)S(1)} %broadcast_multiply_fusion.keep), channel_id=1, source_target_pairs={{0,31},{1,30},{2,29},{3,28},{4,27},{5,26},{6,25},{7,24},{8,23},{9,... | collective-permute-start | bytes 1572872 | tf_op jit(solution)/shard_map/ppermute | solution.py:536
  64.2 40.7 %collective-permute-start.3 = (bf16[256,2048]{1,0:T(8,128)(2,1)}, bf16[256,2048]{1,0:T(8,128)(2,1)S(1)}, u32[]{:S(2)}, u32[]{:S(2)}) collective-permute-start(bf16[256,2048]{1,0:T(8,128)(2,1)} %bitcast.23), channel_id=1, source_target_pairs={{0,32},{32,0},{64,96},{96,64},{1,33},{33,1},{65,97},{97,65},{2,34}... | collective-permute-start | bytes 3145736 | tf_op jit(solution)/shard_map/ppermute | solution.py:540
  71.3 30.3 %collective-permute-start = (bf16[128,2048]{1,0:T(8,128)(2,1)S(1)}, bf16[128,2048]{1,0:T(8,128)(2,1)S(1)}, u32[]{:S(2)}, u32[]{:S(2)}) collective-permute-start(bf16[128,2048]{1,0:T(8,128)(2,1)S(1)} %get-tuple-element.84), channel_id=1, source_target_pairs={{0,31},{1,30},{2,29},{3,28},{4,27},{5,26},{6,25},{7,24},{8,23},{9,... | collective-permute-start | bytes 1572872 | tf_op jit(solution)/shard_map/ppermute | solution.py:536
  80.0 0.8 copy-start.4
  84.1 20.8 %collective-permute-start.2 = (bf16[256,1024]{1,0:T(8,128)(2,1)}, bf16[256,1024]{1,0:T(8,128)(2,1)S(1)}, u32[]{:S(2)}, u32[]{:S(2)}) collective-permute-start(bf16[256,1024]{1,0:T(8,128)(2,1)} %get-tuple-element.51), channel_id=1, source_target_pairs={{0,32},{32,0},{64,96},{96,64},{1,33},{33,1},{65,97},{97,65},{2,34}... | collective-permute-start | bytes 1572872 | tf_op jit(solution)/shard_map/ppermute | solution.py:540
  101.6 0.8 copy-start.3
  104.9 1.0 copy-start.1
  104.9 1.1 copy-start.2
  148.2 46.2 %copy-start.5 = (bf16[2,128,32]{2,1,0:T(8,128)(2,1)S(1)}, bf16[2,128,32]{2,1,0:T(8,128)(2,1)}, u32[]{:S(2)}) copy-start(bf16[2,128,32]{2,1,0:T(8,128)(2,1)} %get-tuple-element.80) | copy-start | bytes 49156

commit v2 on v1

--- a/solution.py
+++ b/solution.py
@@ -110,7 +110,7 @@
     me = lax.axis_index("ctx")
 
     def peer_of(k):
-        return lax.rem(me + k, N_CTX)
+        return lax.rem(me + k * 5, N_CTX)
 
     def state_copy(src, dst, send, recv, strand_at):
         rows = pl.ds(P_SIZE * strand_at, P_SIZE)
@@ -193,10 +193,16 @@
     pl.semaphore_wait(barrier, N_CTX - 1)
 
 
-def forward_exchange(s_ref, dec_ref, out_ref, got_dec, *scratch):
+def forward_exchange(s_ref, dec_ref, proj, run, dt_t, run_t, out_ref, got_dec, local, spread_out, mix_out, *scratch):
     begin, turn, end = scan_steps(False, s_ref, dec_ref, out_ref, got_dec, scratch)
     greet_line()
     begin()
+
+    def block(s, c):
+        local_outputs(s, proj, run, dt_t, run_t, local, spread_out, mix_out)
+        return c
+
+    lax.fori_loop(0, 2, block, 0)
     turn()
     end()
 
@@ -378,9 +384,8 @@
         decay[h] = jnp.broadcast_to(left[h : h + 1, :], (8, 128))
 
 
-def forward_kernel(proj, run, dt_t, run_t, entering, skip, gain, normed, y_out, spread_out, mix_out, local):
-    write, read = proj[0, :, B_AT:C_AT], proj[0, :, C_AT:]
-    affinity = dot(read, write, LANES)
+def local_outputs(s, proj, run, dt_t, run_t, local, spread_out, mix_out):
+    affinity = dot(proj[s, :, C_AT:], proj[s, :, B_AT:C_AT], LANES)
     affinity = jnp.concatenate([affinity, affinity], 1)
     causal = tril()
     left, right = half_masks()
@@ -388,18 +393,21 @@
         cols = slice(DI + 128 * j, DI + 128 * j + 128)
         both = []
         for h in (2 * j, 2 * j + 1):
-            gap = run[0, :, h : h + 1] - run_t[0, h : h + 1, :]
-            both.append(jnp.exp(jnp.where(causal, gap, -1e30)) * dt_t[0, h : h + 1, :])
+            gap = run[s, :, h : h + 1] - run_t[s, h : h + 1, :]
+            both.append(jnp.exp(jnp.where(causal, gap, -1e30)) * dt_t[s, h : h + 1, :])
         spread = jnp.concatenate(both, 1)
-        spread_out[0, j] = spread.astype(bf16)
-        values = proj[0, :, cols]
+        spread_out[s, j] = spread.astype(bf16)
+        values = proj[s, :, cols]
         stacked = jnp.concatenate([values * left, values * right], 0)
         mixing = (spread * affinity).astype(bf16)
-        mix_out[0, j] = mixing
-        local[:, 128 * j : 128 * j + 128] = dot(mixing, stacked)
-    carried = dot(read, entering[...].reshape(DI, NS), LANES)
+        mix_out[s, j] = mixing
+        local[s, :, 128 * j : 128 * j + 128] = dot(mixing, stacked)
+
+
+def forward_kernel(proj, run, local, entering, skip, gain, normed, y_out):
+    carried = dot(proj[0, :, C_AT:], entering[...].reshape(DI, NS), LANES)
     grown = expand(jnp.exp(run[0]), head_map())
-    y = local[...] + grown * carried + skip[...] * proj[0, :, DI:B_AT].astype(f32)
+    y = local[0] + grown * carried + skip[...] * proj[0, :, DI:B_AT].astype(f32)
     y_out[0] = y
     gate = proj[0, :, :DI].astype(f32)
     gated = y * gate * sigmoid(gate)
@@ -554,18 +562,17 @@
          like(f32, 2, H, Q), like(f32, 2, H, Q)],
     )(projections, dt_raw, a_log[None], dt_bias[None])
     states = like(bf16, H, 2 * P_SIZE, NS)
-    entering, decays = exchange_call(
-        forward_exchange, "forward_exchange", 1, [states, like(f32, H, 16, NS)], scan_scratch(), state, factor)
+    entering, decays, local, spread, mixing = exchange_call(
+        forward_exchange, "forward_exchange", 1,
+        [states, like(f32, H, 16, NS), like(f32, 2, Q, DI)] + [like(bf16, 2, PAIRS, Q, 2 * Q)] * 2,
+        scan_scratch(), state, factor, projections, run, dt_t, run_t)
     d_out, grads, grads_away = whole_call(
         flip_kernel, "flip_keep", [like(bf16, 2, Q, DI)] + [like(bf16, 2 * Q, DI // 2)] * 2, keep, got_keep)
     spread_spec = strand(PAIRS, Q, 2 * Q)
-    normed, y, spread, mixing = strand_call(
-        forward_kernel, "forward", [proj, tok, tok_t, tok_t, STATE, lane, lane],
-        [wide, wide, spread_spec, spread_spec],
-        [like(bf16, 2, Q, DI), like(f32, 2, Q, DI), like(bf16, 2, PAIRS, Q, 2 * Q),
-         like(bf16, 2, PAIRS, Q, 2 * Q)],
-        [pltpu.VMEM((Q, DI), f32)],
-    )(projections, run, dt_t, run_t, entering, skip, gain)
+    normed, y = strand_call(
+        forward_kernel, "forward", [proj, tok, wide, STATE, lane, lane], [wide, wide],
+        [like(bf16, 2, Q, DI), like(f32, 2, Q, DI)],
+    )(projections, run, local, entering, skip, gain)
     strand_out = jnp.einsum("srk,dk->srd", normed, w_out, preferred_element_type=f32).astype(bf16)
     moved = mirror(strand_out[1])
     d_normed = jnp.einsum("srd,dk->srk", d_out, w_out, preferred_element_type=f32).astype(bf16)

time: 199 us -> 192 us (0.965)
  starting transfers between devices: 15.6 us -> 10.2 us
    ppermute x2, starting transfers between devices: 15.3 us -> 10 us  [mirror(): lax.ppermute(value, 'ctx', [(i, N_CTX - 1 - i) for i in range(N_CTX)])]
    pallas_call x1, Pallas kernels: 7.11 us -> 4.91 us  [body(): strand_call(forward_kernel, 'forward', [proj, tok, wide, STATE, lane, lan...]
  transfers between devices with their start and end apart: 4 -> 4, of which waited for: 0 -> 0; matrix products, arithmetic and copies ran while one was open for 9% -> 9% of each run, Pallas kernels for 34% -> 35%
where the time goes in v2:
time: 192 us; the launch traced here: 190 us
  Pallas kernels  151 us (79%)
  matrix products  13.1 us (7%)
  local copies, waits for them, and re-layouts  12.3 us (6%)
  starting transfers between devices  10.2 us (5%)
  other arithmetic  3.43 us (2%)
    pallas_call x3, Pallas kernels, exchange_call(): pl.pallas_call(kernel, out_shape=out_shape, in_specs=[vmem] * len(args),...  121 us
    ppermute x2, starting transfers between devices, mirror(): lax.ppermute(value, 'ctx', [(i, N_CTX - 1 - i) for i in range(N_CTX)])  10 us
    pallas_call x1, Pallas kernels, body(): strand_call(backward_kernel, 'backward', [proj, wide, wide, tok, spread_s...  9.17 us
    dot_general x1, matrix products, body(): jnp.einsum('srd,dk->srk', d_out, w_out, preferred_element_type=f32)  7.03 us
    unnamed x15, local copies, waits for them, and re-layouts  6.45 us
    dot_general x1, matrix products, body(): jnp.einsum('srk,dk->srd', normed, w_out, preferred_element_type=f32)  6.08 us
    pallas_call x2, Pallas kernels, whole_call(): pl.pallas_call(kernel, out_shape=out_shape, in_specs=[vmem] * len(args),...  5.81 us
    pallas_call x1, Pallas kernels, body(): strand_call(finish_kernel, 'finish', [proj, tok, tok, tok, STATE, STATE,...  5.64 us
  transfers between devices with their start and end apart: 4, of which 0 were waited for; matrix products, arithmetic and copies ran while one was open for 9% of the time, Pallas kernels for 35%

profile of v2, /device:TPU:4, one launch (start us, length us, event | category | flops | bytes accessed | tf_op | source)
XLA Modules:
  0.0 190.3 jit_solution(11079695722338331805)
XLA Ops:
  0.6 0.7 compare_convert_fusion
  1.3 1.1 broadcast_multiply_fusion.keep
  2.4 0.0 copy-start
  2.5 6.5 %collective-permute-start.1 = (bf16[128,2048]{1,0:T(8,128)(2,1)S(1)}, bf16[128,2048]{1,0:T(8,128)(2,1)S(1)}, u32[]{:S(2)}, u32[]{:S(2)}) collective-permute-start(bf16[128,2048]{1,0:T(8,128)(2,1)S(1)} %broadcast_multiply_fusion.keep), channel_id=1, source_target_pairs={{0,31},{1,30},{2,29},{3,28},{4,27},{5,26},{6,25},{7,24},{8,23},{9,... | collective-permute-start | bytes 1572872 | tf_op jit(solution)/shard_map/ppermute | solution.py:544
  9.0 1.4 copy.21.dt_raw
  10.4 0.7 broadcast_in_dim.20
  11.1 0.7 broadcast_in_dim_reshape.3.skip
  11.8 4.5 %summary.1 = (bf16[32,128,128]{2,1,0:T(8,128)(2,1)}, f32[32,16,128]{2,1,0:T(8,128)}, f32[2,128,32]{2,1,0:T(8,128)}, f32[2,128,32]{2,1,0:T(8,128)}, f32[2,32,128]{2,1,0:T(8,128)}, /*index=5*/f32[2,32,128]{2,1,0:T(8,128)}) custom-call(bf16[2,128,4352]{2,1,0:T(8,128)(2,1)} %proj.9, bf16[2,128,32]{2,1,0:T(8,128)(2,1)} %copy.21.dt_raw, f32[1,32]{1,0:T(1,128)} %bitcast.29, ...), custom_call_target="tpu_custom_call" | custom-call | flops 2000000000 | bytes 10000000 | tf_op jit(solution)/shard_map/summary/pallas_call | solution.py:558
  16.3 0.0 copy-done
  16.3 42.2 %forward_exchange.1 = (bf16[32,128,128]{2,1,0:T(8,128)(2,1)}, f32[32,16,128]{2,1,0:T(8,128)}, f32[2,128,2048]{2,1,0:T(8,128)}, bf16[2,16,128,256]{3,2,1,0:T(8,128)(2,1)}, bf16[2,16,128,256]{3,2,1,0:T(8,128)(2,1)}) custom-call(bf16[32,128,128]{2,1,0:T(8,128)(2,1)} %get-tuple-element.38.s_ref, f32[32,16,128]{2,1,0:T(8,128)} %get-tuple-element.39.dec_ref, ...), custom_call_target="tpu_custom_call" | custom-call | flops 1000000 | bytes 4000000 | tf_op jit(solution)/shard_map/forward_exchange/pallas_call | solution.py:284
  58.5 4.9 %forward.1 = (bf16[2,128,2048]{2,1,0:T(8,128)(2,1)}, f32[2,128,2048]{2,1,0:T(8,128)}) custom-call(bf16[2,128,4352]{2,1,0:T(8,128)(2,1)} %proj.9, f32[2,128,32]{2,1,0:T(8,128)} %get-tuple-element.37.run.run_in, f32[2,128,2048]{2,1,0:T(8,128)} %get-tuple-element.42.local, bf16[32,128,128]{2,1,0:T(8,128)(2,1)} %get-tuple-element.43.entering, ...), custom_call_target="tpu_custom_call" | custom-call | flops 2000000000 | bytes 10000000 | tf_op jit(solution)/shard_map/forward/pallas_call | solution.py:572
  63.4 0.0 collective-permute-start.3
  63.4 6.1 %fusion.4 = bf16[2,128,2048]{2,1,0:T(8,128)(2,1)S(1)} fusion(bf16[2,128,2048]{2,1,0:T(8,128)(2,1)} %get-tuple-element.44, bf16[2048,2048]{1,0:T(8,128)(2,1)} %param.15), kind=kOutput, calls=%fused_computation.4 | convolution fusion | flops 2148007936 | bytes 10485760 | tf_op jit(solution)/shard_map/srk,dk->srd/dot_general | solution.py:576
  69.5 0.9 slice_bitcast_fusion
  70.4 3.5 %collective-permute-start = (bf16[128,2048]{1,0:T(8,128)(2,1)S(1)}, bf16[128,2048]{1,0:T(8,128)(2,1)S(1)}, u32[]{:S(2)}, u32[]{:S(2)}) collective-permute-start(bf16[128,2048]{1,0:T(8,128)(2,1)S(1)} %get-tuple-element.86), channel_id=1, source_target_pairs={{0,31},{1,30},{2,29},{3,28},{4,27},{5,26},{6,25},{7,24},{8,23},{9,... | collective-permute-start | bytes 1572872 | tf_op jit(solution)/shard_map/ppermute | solution.py:544
  73.9 0.0 collective-permute-done.1.got
  73.9 0.0 copy-start.4
  73.9 0.8 copy-done.4
  74.7 3.3 %flip_keep.1 = (bf16[2,128,2048]{2,1,0:T(8,128)(2,1)}, bf16[256,1024]{1,0:T(8,128)(2,1)}, bf16[256,1024]{1,0:T(8,128)(2,1)}) custom-call(bf16[128,2048]{1,0:T(8,128)(2,1)} %copy-done, bf16[128,2048]{1,0:T(8,128)(2,1)} %copy-done.4), custom_call_target="tpu_custom_call" | custom-call | flops 200000000 | bytes 2000000 | tf_op jit(solution)/shard_map/flip_keep/pallas_call | solution.py:538
  78.0 0.2 collective-permute-start.2
  78.2 7.0 %fusion.7.d_normed = bf16[2,128,2048]{2,1,0:T(8,128)(2,1)} fusion(bf16[2,128,2048]{2,1,0:T(8,128)(2,1)} %get-tuple-element.47, bf16[2048,2048]{1,0:T(8,128)(2,1)} %param.15), kind=kOutput, calls=%fused_computation.5 | convolution fusion | flops 2148007936 | bytes 10485760 | tf_op jit(solution)/shard_map/srd,dk->srk/dot_general | solution.py:578
  85.2 9.2 %backward.1 = (bf16[2,128,2048]{2,1,0:T(8,128)(2,1)}, f32[2,128,2048]{2,1,0:T(8,128)}, bf16[32,128,128]{2,1,0:T(8,128)(2,1)}, f32[2,128,128]{2,1,0:T(8,128)}, bf...) custom-call(bf16[2,128,4352]{2,1,0:T(8,128)(2,1)} %proj.9, ...), custom_call_target="tpu_custom_call" | custom-call | flops 2000000000 | bytes 10000000 | tf_op jit(solution)/shard_map/backward/pallas_call | solution.py:579
  94.4 0.8 reduce_sum.27
  95.2 0.1 reshape_squeeze.3
  95.3 0.1 reduce_sum.29
  95.4 0.0 collective-permute-done.got
  95.4 0.0 copy-start.3
  95.4 0.8 copy-done.3
  96.2 2.6 %mix.1 = bf16[128,2048]{1,0:T(8,128)(2,1)} custom-call(bf16[128,2048]{1,0:T(8,128)(2,1)} %get-tuple-element.87.own, bf16[128,2048]{1,0:T(8,128)(2,1)} %copy-done.3), custom_call_target="tpu_custom_call" | custom-call | flops 200000000 | bytes 2000000 | tf_op jit(solution)/shard_map/mix/pallas_call | solution.py:538
  98.7 0.0 collective-permute-done.3.normed_other
  98.7 0.0 copy-start.1
  98.8 0.0 collective-permute-done.2.grads_other
  98.8 0.0 copy-start.2
  98.8 1.0 copy-done.1
  99.7 0.2 copy-done.2
  99.9 39.2 %backward_exchange.1 = (bf16[32,128,128]{2,1,0:T(8,128)(2,1)}, bf16[4,4,4,16,2048]{4,3,2,1,0:T(8,128)(2,1)}) custom-call(bf16[32,128,128]{2,1,0:T(8,128)(2,1)} %get-tuple-element.50.s_ref, f32[32,16,128]{2,1,0:T(8,128)} %get-tuple-element.51.dec_ref, bf16[256,1024]{1,0:T(8,128)(2,1)} %get-tuple-element.52.grads, bf16[256,1024]{1,0:T(8,128)(2,1)} %copy-done.2, ...), custom_call_target="tpu_custom_call" | custom-call | flops 1000000 | bytes 4000000 | tf_op jit(solution)/shard_map/backward_exchange/pallas_call | solution.py:284
  139.1 5.6 %finish.1 = (bf16[2,128,4352]{2,1,0:T(8,128)(2,1)}, bf16[2,128,32]{2,1,0:T(8,128)(2,1)}, f32[2,2,32]{2,1,0:T(2,128)}) custom-call(bf16[2,128,4352]{2,1,0:T(8,128)(2,1)} %proj.9, bf16[2,128,32]{2,1,0:T(8,128)(2,1)} %copy.21.dt_raw, f32[2,128,32]{2,1,0:T(8,128)} %get-tuple-element.45.dt_in, f32[2,128,32]{2,1,0:T(8,128)} %get-tuple-element.37.run.run_in, ...), custom_call_target="tpu_custom_call" | custom-call | flops 2000000000 | bytes 10000000 | tf_op jit(solution)/shard_map/finish/pallas_call | solution.py:591
  144.8 0.0 copy-start.5
  144.8 0.7 reduce_sum.28
  145.5 0.1 reshape.28
  145.6 0.7 concatenate.3
  146.3 39.1 %last_exchange.1 = (f32[24,128]{1,0:T(8,128)}, f32[16,2048]{1,0:T(8,128)}) custom-call(f32[24,128]{1,0:T(8,128)} %bitcast.25, bf16[4,4,4,16,2048]{4,3,2,1,0:T(8,128)(2,1)} %get-tuple-element.65.weight), custom_call_target="tpu_custom_call" | custom-call | flops 1000000 | bytes 4000000 | tf_op jit(solution)/shard_map/last_exchange/pallas_call | solution.py:284
  185.4 0.8 slice.28
  186.2 1.3 slice_bitcast_fusion.2
  187.5 0.6 slice.36
  188.0 0.0 copy-done.5
  188.0 0.7 copy.23
  188.7 1.6 copy.25
  (2 shorter events, 0.0 us)
Async XLA Ops:
  2.4 13.8 %copy-start = (bf16[128,2048]{1,0:T(8,128)(2,1)}, bf16[128,2048]{1,0:T(8,128)(2,1)S(1)}, u32[]{:S(2)}) copy-start(bf16[128,2048]{1,0:T(8,128)(2,1)S(1)} %broadcast_multiply_fusion.keep) | copy-start | bytes 1572868
  2.5 71.4 %collective-permute-start.1 = (bf16[128,2048]{1,0:T(8,128)(2,1)S(1)}, bf16[128,2048]{1,0:T(8,128)(2,1)S(1)}, u32[]{:S(2)}, u32[]{:S(2)}) collective-permute-start(bf16[128,2048]{1,0:T(8,128)(2,1)S(1)} %broadcast_multiply_fusion.keep), channel_id=1, source_target_pairs={{0,31},{1,30},{2,29},{3,28},{4,27},{5,26},{6,25},{7,24},{8,23},{9,... | collective-permute-start | bytes 1572872 | tf_op jit(solution)/shard_map/ppermute | solution.py:544
  63.4 35.4 %collective-permute-start.3 = (bf16[256,2048]{1,0:T(8,128)(2,1)}, bf16[256,2048]{1,0:T(8,128)(2,1)S(1)}, u32[]{:S(2)}, u32[]{:S(2)}) collective-permute-start(bf16[256,2048]{1,0:T(8,128)(2,1)} %bitcast.23), channel_id=1, source_target_pairs={{0,32},{32,0},{64,96},{96,64},{1,33},{33,1},{65,97},{97,65},{2,34}... | collective-permute-start | bytes 3145736 | tf_op jit(solution)/shard_map/ppermute | solution.py:548
  70.4 25.0 %collective-permute-start = (bf16[128,2048]{1,0:T(8,128)(2,1)S(1)}, bf16[128,2048]{1,0:T(8,128)(2,1)S(1)}, u32[]{:S(2)}, u32[]{:S(2)}) collective-permute-start(bf16[128,2048]{1,0:T(8,128)(2,1)S(1)} %get-tuple-element.86), channel_id=1, source_target_pairs={{0,31},{1,30},{2,29},{3,28},{4,27},{5,26},{6,25},{7,24},{8,23},{9,... | collective-permute-start | bytes 1572872 | tf_op jit(solution)/shard_map/ppermute | solution.py:544
  73.9 0.8 copy-start.4
  78.0 20.8 %collective-permute-start.2 = (bf16[256,1024]{1,0:T(8,128)(2,1)}, bf16[256,1024]{1,0:T(8,128)(2,1)S(1)}, u32[]{:S(2)}, u32[]{:S(2)}) collective-permute-start(bf16[256,1024]{1,0:T(8,128)(2,1)} %get-tuple-element.53), channel_id=1, source_target_pairs={{0,32},{32,0},{64,96},{96,64},{1,33},{33,1},{65,97},{97,65},{2,34}... | collective-permute-start | bytes 1572872 | tf_op jit(solution)/shard_map/ppermute | solution.py:548
  95.4 0.8 copy-start.3
  98.7 1.0 copy-start.1
  98.8 1.1 copy-start.2
  144.8 43.3 %copy-start.5 = (bf16[2,128,32]{2,1,0:T(8,128)(2,1)S(1)}, bf16[2,128,32]{2,1,0:T(8,128)(2,1)}, u32[]{:S(2)}) copy-start(bf16[2,128,32]{2,1,0:T(8,128)(2,1)} %get-tuple-element.82) | copy-start | bytes 49156

commit v3 on v2

--- a/solution.py
+++ b/solution.py
@@ -113,7 +113,7 @@
         return lax.rem(me + k * 5, N_CTX)
 
     def state_copy(src, dst, send, recv, strand_at):
-        rows = pl.ds(P_SIZE * strand_at, P_SIZE)
+        rows = pl.ds(0, 2 * P_SIZE)
 
         def make(k):
             return pltpu.make_async_remote_copy(
@@ -127,8 +127,8 @@
             src_ref=dec_ref.at[peer_of(k)], dst_ref=got_dec.at[me], send_sem=send_d.at[k], recv_sem=recv_d.at[k],
             device_id={"ctx": peer_of(k)}, device_id_type=MESH)
 
-    copy_a = [state_copy(s_ref, got, send_a, recv_a, i) for i in range(2)]
-    copy_b = [state_copy(pre, out_ref, send_b, recv_b, i) for i in range(2)]
+    copy_a = state_copy(s_ref, got, send_a, recv_a, 0)
+    copy_b = state_copy(pre, out_ref, send_b, recv_b, 0)
 
     def start(make):
         def step(k, c):
@@ -145,8 +145,7 @@
     def begin():
         if not backward:
             start(copy_d)
-        for i in range(2):
-            start(copy_a[i])
+        start(copy_a)
         own = pltpu.make_async_copy(s_ref.at[me], got.at[me], own_sem.at[0])
         own.start()
         own.wait()
@@ -159,8 +158,8 @@
         if not backward:
             finish(copy_d)
         decays = dec_ref if backward else got_dec
+        finish(copy_a)
         for i in range(2):
-            finish(copy_a[i])
             rows = slice(P_SIZE * i, P_SIZE * i + P_SIZE)
 
             def fold(n, carry, i=i, rows=rows):
@@ -169,14 +168,13 @@
                 return decays[at, 8 * i : 8 * i + 1, :] * carry + got[at, rows, :].astype(jnp.float32)
 
             lax.fori_loop(0, N_CTX, fold, jnp.zeros((P_SIZE, NS), jnp.float32))
-            start(copy_b[i])
+        start(copy_b)
 
     def end():
         own = pltpu.make_async_copy(pre.at[me], out_ref.at[me], own_sem.at[2])
         own.start()
         own.wait()
-        for i in range(2):
-            finish(copy_b[i])
+        finish(copy_b)
 
     return begin, turn, end
 

time: 192 us -> 198 us (1.031)
  Pallas kernels: 151 us -> 155 us
    pallas_call x3, Pallas kernels: 121 us -> 125 us  [exchange_call(): pl.pallas_call(kernel, out_shape=out_shape, in_specs=[vmem] * len(args),...]
where the time goes in v3:
time: 198 us; the launch traced here: 197 us
  Pallas kernels  155 us (78%)
  matrix products  13.1 us (7%)
  local copies, waits for them, and re-layouts  12.3 us (6%)
  starting transfers between devices  12 us (6%)
  other arithmetic  3.43 us (2%)
    pallas_call x3, Pallas kernels, exchange_call(): pl.pallas_call(kernel, out_shape=out_shape, in_specs=[vmem] * len(args),...  125 us
    ppermute x2, starting transfers between devices, mirror(): lax.ppermute(value, 'ctx', [(i, N_CTX - 1 - i) for i in range(N_CTX)])  11.8 us
    pallas_call x1, Pallas kernels, body(): strand_call(backward_kernel, 'backward', [proj, wide, wide, tok, spread_s...  9.17 us
    dot_general x1, matrix products, body(): jnp.einsum('srd,dk->srk', d_out, w_out, preferred_element_type=f32)  7.03 us
    unnamed x15, local copies, waits for them, and re-layouts  6.45 us
    dot_general x1, matrix products, body(): jnp.einsum('srk,dk->srd', normed, w_out, preferred_element_type=f32)  6.08 us
    pallas_call x2, Pallas kernels, whole_call(): pl.pallas_call(kernel, out_shape=out_shape, in_specs=[vmem] * len(args),...  5.81 us
    pallas_call x1, Pallas kernels, body(): strand_call(finish_kernel, 'finish', [proj, tok, tok, tok, STATE, STATE,...  5.64 us
  transfers between devices with their start and end apart: 4, of which 0 were waited for; matrix products, arithmetic and copies ran while one was open for 9% of the time, Pallas kernels for 35%

profile of v3, /device:TPU:4, one launch (start us, length us, event | category | flops | bytes accessed | tf_op | source)
XLA Modules:
  0.0 196.6 jit_solution(17687113054911813715)
XLA Ops:
  0.6 0.7 compare_convert_fusion
  1.3 1.1 broadcast_multiply_fusion.keep
  2.4 0.0 copy-start
  2.5 6.5 %collective-permute-start.1 = (bf16[128,2048]{1,0:T(8,128)(2,1)S(1)}, bf16[128,2048]{1,0:T(8,128)(2,1)S(1)}, u32[]{:S(2)}, u32[]{:S(2)}) collective-permute-start(bf16[128,2048]{1,0:T(8,128)(2,1)S(1)} %broadcast_multiply_fusion.keep), channel_id=1, source_target_pairs={{0,31},{1,30},{2,29},{3,28},{4,27},{5,26},{6,25},{7,24},{8,23},{9,... | collective-permute-start | bytes 1572872 | tf_op jit(solution)/shard_map/ppermute | solution.py:542
  9.0 1.4 copy.21.dt_raw
  10.4 0.7 broadcast_in_dim.20
  11.1 0.7 broadcast_in_dim_reshape.3.skip
  11.8 4.5 %summary.1 = (bf16[32,128,128]{2,1,0:T(8,128)(2,1)}, f32[32,16,128]{2,1,0:T(8,128)}, f32[2,128,32]{2,1,0:T(8,128)}, f32[2,128,32]{2,1,0:T(8,128)}, f32[2,32,128]{2,1,0:T(8,128)}, /*index=5*/f32[2,32,128]{2,1,0:T(8,128)}) custom-call(bf16[2,128,4352]{2,1,0:T(8,128)(2,1)} %proj.9, bf16[2,128,32]{2,1,0:T(8,128)(2,1)} %copy.21.dt_raw, f32[1,32]{1,0:T(1,128)} %bitcast.29, ...), custom_call_target="tpu_custom_call" | custom-call | flops 2000000000 | bytes 10000000 | tf_op jit(solution)/shard_map/summary/pallas_call | solution.py:556
  16.3 0.0 copy-done
  16.3 44.3 %forward_exchange.1 = (bf16[32,128,128]{2,1,0:T(8,128)(2,1)}, f32[32,16,128]{2,1,0:T(8,128)}, f32[2,128,2048]{2,1,0:T(8,128)}, bf16[2,16,128,256]{3,2,1,0:T(8,128)(2,1)}, bf16[2,16,128,256]{3,2,1,0:T(8,128)(2,1)}) custom-call(bf16[32,128,128]{2,1,0:T(8,128)(2,1)} %get-tuple-element.38.s_ref, f32[32,16,128]{2,1,0:T(8,128)} %get-tuple-element.39.dec_ref, ...), custom_call_target="tpu_custom_call" | custom-call | flops 1000000 | bytes 4000000 | tf_op jit(solution)/shard_map/forward_exchange/pallas_call | solution.py:282
  60.6 4.9 %forward.1 = (bf16[2,128,2048]{2,1,0:T(8,128)(2,1)}, f32[2,128,2048]{2,1,0:T(8,128)}) custom-call(bf16[2,128,4352]{2,1,0:T(8,128)(2,1)} %proj.9, f32[2,128,32]{2,1,0:T(8,128)} %get-tuple-element.37.run.run_in, f32[2,128,2048]{2,1,0:T(8,128)} %get-tuple-element.42.local, bf16[32,128,128]{2,1,0:T(8,128)(2,1)} %get-tuple-element.43.entering, ...), custom_call_target="tpu_custom_call" | custom-call | flops 2000000000 | bytes 10000000 | tf_op jit(solution)/shard_map/forward/pallas_call | solution.py:570
  65.5 0.0 collective-permute-start.3
  65.5 6.1 %fusion.4 = bf16[2,128,2048]{2,1,0:T(8,128)(2,1)S(1)} fusion(bf16[2,128,2048]{2,1,0:T(8,128)(2,1)} %get-tuple-element.44, bf16[2048,2048]{1,0:T(8,128)(2,1)} %param.15), kind=kOutput, calls=%fused_computation.4 | convolution fusion | flops 2148007936 | bytes 10485760 | tf_op jit(solution)/shard_map/srk,dk->srd/dot_general | solution.py:574
  71.6 0.9 slice_bitcast_fusion
  72.5 5.3 %collective-permute-start = (bf16[128,2048]{1,0:T(8,128)(2,1)S(1)}, bf16[128,2048]{1,0:T(8,128)(2,1)S(1)}, u32[]{:S(2)}, u32[]{:S(2)}) collective-permute-start(bf16[128,2048]{1,0:T(8,128)(2,1)S(1)} %get-tuple-element.86), channel_id=1, source_target_pairs={{0,31},{1,30},{2,29},{3,28},{4,27},{5,26},{6,25},{7,24},{8,23},{9,... | collective-permute-start | bytes 1572872 | tf_op jit(solution)/shard_map/ppermute | solution.py:542
  77.7 0.0 collective-permute-done.1.got
  77.7 0.0 copy-start.4
  77.7 0.8 copy-done.4
  78.6 3.3 %flip_keep.1 = (bf16[2,128,2048]{2,1,0:T(8,128)(2,1)}, bf16[256,1024]{1,0:T(8,128)(2,1)}, bf16[256,1024]{1,0:T(8,128)(2,1)}) custom-call(bf16[128,2048]{1,0:T(8,128)(2,1)} %copy-done, bf16[128,2048]{1,0:T(8,128)(2,1)} %copy-done.4), custom_call_target="tpu_custom_call" | custom-call | flops 200000000 | bytes 2000000 | tf_op jit(solution)/shard_map/flip_keep/pallas_call | solution.py:536
  81.8 0.2 collective-permute-start.2
  82.0 7.0 %fusion.7.d_normed = bf16[2,128,2048]{2,1,0:T(8,128)(2,1)} fusion(bf16[2,128,2048]{2,1,0:T(8,128)(2,1)} %get-tuple-element.47, bf16[2048,2048]{1,0:T(8,128)(2,1)} %param.15), kind=kOutput, calls=%fused_computation.5 | convolution fusion | flops 2148007936 | bytes 10485760 | tf_op jit(solution)/shard_map/srd,dk->srk/dot_general | solution.py:576
  89.1 9.2 %backward.1 = (bf16[2,128,2048]{2,1,0:T(8,128)(2,1)}, f32[2,128,2048]{2,1,0:T(8,128)}, bf16[32,128,128]{2,1,0:T(8,128)(2,1)}, f32[2,128,128]{2,1,0:T(8,128)}, bf...) custom-call(bf16[2,128,4352]{2,1,0:T(8,128)(2,1)} %proj.9, ...), custom_call_target="tpu_custom_call" | custom-call | flops 2000000000 | bytes 10000000 | tf_op jit(solution)/shard_map/backward/pallas_call | solution.py:577
  98.2 0.8 reduce_sum.27
  99.1 0.1 reshape_squeeze.3
  99.1 0.1 reduce_sum.29
  99.2 0.0 collective-permute-done.got
  99.3 0.0 copy-start.3
  99.3 0.8 copy-done.3
  100.0 2.6 %mix.1 = bf16[128,2048]{1,0:T(8,128)(2,1)} custom-call(bf16[128,2048]{1,0:T(8,128)(2,1)} %get-tuple-element.87.own, bf16[128,2048]{1,0:T(8,128)(2,1)} %copy-done.3), custom_call_target="tpu_custom_call" | custom-call | flops 200000000 | bytes 2000000 | tf_op jit(solution)/shard_map/mix/pallas_call | solution.py:536
  102.6 0.0 collective-permute-done.3.normed_other
  102.6 0.0 copy-start.1
  102.6 0.0 collective-permute-done.2.grads_other
  102.6 0.0 copy-start.2
  102.6 1.0 copy-done.1
  103.6 0.2 copy-done.2
  103.8 42.4 %backward_exchange.1 = (bf16[32,128,128]{2,1,0:T(8,128)(2,1)}, bf16[4,4,4,16,2048]{4,3,2,1,0:T(8,128)(2,1)}) custom-call(bf16[32,128,128]{2,1,0:T(8,128)(2,1)} %get-tuple-element.50.s_ref, f32[32,16,128]{2,1,0:T(8,128)} %get-tuple-element.51.dec_ref, bf16[256,1024]{1,0:T(8,128)(2,1)} %get-tuple-element.52.grads, bf16[256,1024]{1,0:T(8,128)(2,1)} %copy-done.2, ...), custom_call_target="tpu_custom_call" | custom-call | flops 1000000 | bytes 4000000 | tf_op jit(solution)/shard_map/backward_exchange/pallas_call | solution.py:282
  146.1 5.6 %finish.1 = (bf16[2,128,4352]{2,1,0:T(8,128)(2,1)}, bf16[2,128,32]{2,1,0:T(8,128)(2,1)}, f32[2,2,32]{2,1,0:T(2,128)}) custom-call(bf16[2,128,4352]{2,1,0:T(8,128)(2,1)} %proj.9, bf16[2,128,32]{2,1,0:T(8,128)(2,1)} %copy.21.dt_raw, f32[2,128,32]{2,1,0:T(8,128)} %get-tuple-element.45.dt_in, f32[2,128,32]{2,1,0:T(8,128)} %get-tuple-element.37.run.run_in, ...), custom_call_target="tpu_custom_call" | custom-call | flops 2000000000 | bytes 10000000 | tf_op jit(solution)/shard_map/finish/pallas_call | solution.py:589
  151.8 0.0 copy-start.5
  151.8 0.7 reduce_sum.28
  152.5 0.1 reshape.28
  152.6 0.7 concatenate.3
  153.3 38.4 %last_exchange.1 = (f32[24,128]{1,0:T(8,128)}, f32[16,2048]{1,0:T(8,128)}) custom-call(f32[24,128]{1,0:T(8,128)} %bitcast.25, bf16[4,4,4,16,2048]{4,3,2,1,0:T(8,128)(2,1)} %get-tuple-element.65.weight), custom_call_target="tpu_custom_call" | custom-call | flops 1000000 | bytes 4000000 | tf_op jit(solution)/shard_map/last_exchange/pallas_call | solution.py:282
  191.6 0.8 slice.28
  192.4 1.3 slice_bitcast_fusion.2
  193.7 0.6 slice.36
  194.3 0.0 copy-done.5
  194.3 0.7 copy.23
  195.0 1.6 copy.25
  (2 shorter events, 0.0 us)
Async XLA Ops:
  2.4 13.8 %copy-start = (bf16[128,2048]{1,0:T(8,128)(2,1)}, bf16[128,2048]{1,0:T(8,128)(2,1)S(1)}, u32[]{:S(2)}) copy-start(bf16[128,2048]{1,0:T(8,128)(2,1)S(1)} %broadcast_multiply_fusion.keep) | copy-start | bytes 1572868
  2.5 75.3 %collective-permute-start.1 = (bf16[128,2048]{1,0:T(8,128)(2,1)S(1)}, bf16[128,2048]{1,0:T(8,128)(2,1)S(1)}, u32[]{:S(2)}, u32[]{:S(2)}) collective-permute-start(bf16[128,2048]{1,0:T(8,128)(2,1)S(1)} %broadcast_multiply_fusion.keep), channel_id=1, source_target_pairs={{0,31},{1,30},{2,29},{3,28},{4,27},{5,26},{6,25},{7,24},{8,23},{9,... | collective-permute-start | bytes 1572872 | tf_op jit(solution)/shard_map/ppermute | solution.py:542
  65.5 37.1 %collective-permute-start.3 = (bf16[256,2048]{1,0:T(8,128)(2,1)}, bf16[256,2048]{1,0:T(8,128)(2,1)S(1)}, u32[]{:S(2)}, u32[]{:S(2)}) collective-permute-start(bf16[256,2048]{1,0:T(8,128)(2,1)} %bitcast.23), channel_id=1, source_target_pairs={{0,32},{32,0},{64,96},{96,64},{1,33},{33,1},{65,97},{97,65},{2,34}... | collective-permute-start | bytes 3145736 | tf_op jit(solution)/shard_map/ppermute | solution.py:546
  72.5 26.8 %collective-permute-start = (bf16[128,2048]{1,0:T(8,128)(2,1)S(1)}, bf16[128,2048]{1,0:T(8,128)(2,1)S(1)}, u32[]{:S(2)}, u32[]{:S(2)}) collective-permute-start(bf16[128,2048]{1,0:T(8,128)(2,1)S(1)} %get-tuple-element.86), channel_id=1, source_target_pairs={{0,31},{1,30},{2,29},{3,28},{4,27},{5,26},{6,25},{7,24},{8,23},{9,... | collective-permute-start | bytes 1572872 | tf_op jit(solution)/shard_map/ppermute | solution.py:542
  77.7 0.8 copy-start.4
  81.8 20.8 %collective-permute-start.2 = (bf16[256,1024]{1,0:T(8,128)(2,1)}, bf16[256,1024]{1,0:T(8,128)(2,1)S(1)}, u32[]{:S(2)}, u32[]{:S(2)}) collective-permute-start(bf16[256,1024]{1,0:T(8,128)(2,1)} %get-tuple-element.53), channel_id=1, source_target_pairs={{0,32},{32,0},{64,96},{96,64},{1,33},{33,1},{65,97},{97,65},{2,34}... | collective-permute-start | bytes 1572872 | tf_op jit(solution)/shard_map/ppermute | solution.py:546
  99.3 0.8 copy-start.3
  102.6 1.0 copy-start.1
  102.6 1.1 copy-start.2
  151.8 42.5 %copy-start.5 = (bf16[2,128,32]{2,1,0:T(8,128)(2,1)S(1)}, bf16[2,128,32]{2,1,0:T(8,128)(2,1)}, u32[]{:S(2)}) copy-start(bf16[2,128,32]{2,1,0:T(8,128)(2,1)} %get-tuple-element.82) | copy-start | bytes 49156
